TPU v7x, 32 devices: a whole 2x2x4 slice. The times are simulated.
32 devices in a mesh: groups: 2 (over y), blk: 4 (over x, core), req: 4 (over z).
Axes of the slice: x: 2, y: 2, z: 4, core: 2. Of those that a mesh axis runs over, the one named last changes fastest.
Arguments:
- hidden_states: bfloat16 [640, 4608], P(('groups', 'req'), 'blk'), parts along dimension 0, may hold values from -12 to 12
- context_lengths: int32 [128], P(('groups', 'req')), parts along dimension 0, may hold values from 64 to 512
- cache_keys: bfloat16 [128, 512, 16, 128], P(('groups', 'req'), None, 'blk'), parts along dimension 0, may hold values from -1400 to 1400
- cache_values: bfloat16 [128, 512, 16, 128], P(('groups', 'req'), None, 'blk'), parts along dimension 0, may hold values from -6 to 6
- q_weight: bfloat16 [4608, 4096], P('req', 'blk'), may hold values from -0.09375 to 0.09375
- k_weight: bfloat16 [4608, 2048], P('req', 'blk'), may hold values from -0.09375 to 0.09375
- v_weight: bfloat16 [4608, 2048], P('req', 'blk'), may hold values from -0.09375 to 0.09375
- o_weight: bfloat16 [4096, 4608], P('blk'), may hold values from -1 to 1
- gate_weight: bfloat16 [18432, 4608], P(('blk', 'req')), may hold values from -0.09375 to 0.09375
- up_weight: bfloat16 [18432, 4608], P(('blk', 'req')), may hold values from -0.09375 to 0.09375
- down_weight: bfloat16 [18432, 4608], P(('blk', 'req')), may hold values from -0.0625 to 0.0625
- attn_gain: float32 [4608], P('blk'), may hold values from 0.1 to 1.9
- post_attn_gain: float32 [4608], P('blk'), may hold values from 0.1 to 1.9
- ffn_gain: float32 [4608], P('blk'), may hold values from 0.1 to 1.9
- post_ffn_gain: float32 [4608], P('blk'), may hold values from 0.1 to 1.9
Outputs:
- layer_output: bfloat16 [640, 4608], P(('groups', 'req'), 'blk'), parts along dimension 0
- draft_keys: bfloat16 [128, 5, 16, 128], P(('groups', 'req'), None, 'blk'), parts along dimension 0
- draft_values: bfloat16 [128, 5, 16, 128], P(('groups', 'req'), None, 'blk'), parts along dimension 0
There are 2 independent parts, one for each index of `groups`. A program takes and returns all parts, laid end to end along the dimension named above; an argument that names none is the same for every part. Nothing has to cross between parts.
All inputs are finite; a program needn't handle non-finite values.
Results may differ from a plain program's by a relative error of at most 0.015.
Values may be sent and summed in bfloat16 or wider, within the bound.
A program may use at most 128 MiB of HBM per device.

v0:
```python
import jax
import jax.numpy as jnp
from jax import lax
from jax.sharding import PartitionSpec as P

D = 4608
HEADS = 32


EPSILON = 1e-06
NEGATIVE = -1e30


def rotate(values, positions):
    size = values.shape[-1]
    half = size // 2
    rates = 10000.0 ** (-(jnp.arange(half, dtype=jnp.float32) * 2.0) / size)
    angle = positions.astype(jnp.float32)[..., None] * rates
    cosine = jnp.cos(angle)
    sine = jnp.sin(angle)
    first = values[..., :half]
    second = values[..., half:]
    return jnp.concatenate(
        [first * cosine - second * sine, second * cosine + first * sine], axis=-1
    )


def scaling(total):
    return lax.rsqrt(total / D + EPSILON)[:, None]


def attend(queries, new_keys, new_values, cache_keys, cache_values, lengths):
    req_count, steps, heads, size = queries.shape
    shared = new_keys.shape[2]
    group = heads // shared
    scale = (D // HEADS) ** (-0.5)
    grouped = queries.reshape(req_count, steps, shared, group, size)
    older = (
        jnp.einsum("rskge,rcke->rkgsc", grouped, cache_keys, preferred_element_type=jnp.float32)
        * scale
    )
    newer = (
        jnp.einsum("rskge,rtke->rkgst", grouped, new_keys, preferred_element_type=jnp.float32)
        * scale
    )
    valid = jnp.arange(cache_keys.shape[1], dtype=jnp.int32)[None, :] < lengths[:, None]
    older = jnp.where(valid[:, None, None, None, :], older, NEGATIVE)
    causal = (
        jnp.arange(steps, dtype=jnp.int32)[:, None] >= jnp.arange(steps, dtype=jnp.int32)[None, :]
    )
    newer = jnp.where(causal, newer, NEGATIVE)
    highest = jnp.maximum(jnp.max(older, axis=-1), jnp.max(newer, axis=-1))[..., None]
    far_mass = jnp.exp(older - highest)
    near_mass = jnp.exp(newer - highest)
    total_mass = (jnp.sum(far_mass, axis=-1) + jnp.sum(near_mass, axis=-1))[..., None]
    far_weights = (far_mass / total_mass).astype(jnp.bfloat16)
    near_weights = (near_mass / total_mass).astype(jnp.bfloat16)
    blended = jnp.einsum(
        "rkgsc,rcke->rskge", far_weights, cache_values, preferred_element_type=jnp.float32
    )
    blended = blended + jnp.einsum(
        "rkgst,rtke->rskge", near_weights, new_values, preferred_element_type=jnp.float32
    )
    return blended.reshape(req_count * steps, heads * size).astype(jnp.bfloat16)


def body(
    hidden_states,
    context_lengths,
    cache_keys,
    cache_values,
    q_weight,
    k_weight,
    v_weight,
    o_weight,
    gate_weight,
    up_weight,
    down_weight,
    attn_gain,
    post_attn_gain,
    ffn_gain,
    post_ffn_gain,
):
    token_rows = hidden_states.shape[0]
    req_count = context_lengths.shape[0]
    steps = token_rows // req_count
    kv_local = cache_keys.shape[2]
    size = cache_keys.shape[3]
    query_cols = q_weight.shape[1]
    key_cols = k_weight.shape[1]
    heads_local = query_cols // size
    states = hidden_states.astype(jnp.float32)
    total = lax.psum(jnp.sum(states * states, axis=1), "blk")
    normed = (states * scaling(total) * attn_gain).astype(jnp.bfloat16)
    whole = lax.all_gather(normed, "blk", axis=1, tiled=True)
    slices = lax.all_to_all(whole, "req", split_axis=1, concat_axis=0, tiled=True)
    joined = lax.psum_scatter(
        jnp.concatenate(
            [
                jnp.dot(slices, q_weight, preferred_element_type=jnp.float32),
                jnp.dot(slices, k_weight, preferred_element_type=jnp.float32),
                jnp.dot(slices, v_weight, preferred_element_type=jnp.float32),
            ],
            axis=1,
        ),
        "req",
        scatter_dimension=0,
        tiled=True,
    )
    query_lin = joined[:, :query_cols]
    key_lin = joined[:, query_cols : query_cols + key_cols]
    value_lin = joined[:, query_cols + key_cols :]
    positions = (context_lengths[:, None] + jnp.arange(steps, dtype=jnp.int32)[None, :]).reshape(
        token_rows
    )
    queries = rotate(query_lin.reshape(token_rows, heads_local, size), positions[:, None]).astype(
        jnp.bfloat16
    )
    new_keys = rotate(key_lin.reshape(token_rows, kv_local, size), positions[:, None]).astype(
        jnp.bfloat16
    )
    draft_keys = new_keys.reshape(req_count, steps, kv_local, size)
    draft_values = value_lin.astype(jnp.bfloat16).reshape(req_count, steps, kv_local, size)
    attended = attend(
        queries.reshape(req_count, steps, heads_local, size),
        draft_keys,
        draft_values,
        cache_keys,
        cache_values,
        context_lengths,
    )
    mixed = (
        lax.psum_scatter(
            lax.dot_general(
                o_weight, attended, (((0,), (1,)), ((), ())), preferred_element_type=jnp.float32
            ).astype(jnp.bfloat16),
            "blk",
            scatter_dimension=0,
            tiled=True,
        )
        .astype(jnp.float32)
        .T
    )
    total = lax.psum(jnp.sum(mixed * mixed, axis=1), "blk")
    middle = (states + mixed * scaling(total) * post_attn_gain).astype(jnp.bfloat16)
    middle_wide = middle.astype(jnp.float32)
    total = lax.psum(jnp.sum(middle_wide * middle_wide, axis=1), "blk")
    normed_mid = (middle_wide * scaling(total) * ffn_gain).astype(jnp.bfloat16)
    features = lax.all_gather(normed_mid, "blk", axis=1, tiled=True)
    piece = lax.all_gather(features, "req", axis=0, tiled=True)
    gate = lax.dot_general(
        piece, gate_weight, (((1,), (1,)), ((), ())), preferred_element_type=jnp.float32
    )
    up = lax.dot_general(
        piece, up_weight, (((1,), (1,)), ((), ())), preferred_element_type=jnp.float32
    )
    terms = lax.dot_general(
        down_weight,
        (jax.nn.gelu(gate, approximate=True) * up).astype(jnp.bfloat16),
        (((0,), (1,)), ((), ())),
        preferred_element_type=jnp.float32,
    )
    partial_sum = lax.psum_scatter(
        terms.astype(jnp.bfloat16), "blk", scatter_dimension=0, tiled=True
    )
    ffn_out = (
        lax.psum_scatter(partial_sum, "req", scatter_dimension=1, tiled=True).astype(jnp.float32).T
    )
    total = lax.psum(jnp.sum(ffn_out * ffn_out, axis=1), "blk")
    layer_output = (middle_wide + ffn_out * scaling(total) * post_ffn_gain).astype(jnp.bfloat16)
    return (layer_output, draft_keys, draft_values)


def solution(mesh):
    placed = (
        P(("groups", "req"), "blk"),
        P(("groups", "req")),
        P(("groups", "req"), None, "blk", None),
        P(("groups", "req"), None, "blk", None),
        P("req", "blk"),
        P("req", "blk"),
        P("req", "blk"),
        P("blk", None),
        P(("blk", "req"), None),
        P(("blk", "req"), None),
        P(("blk", "req"), None),
        P("blk"),
        P("blk"),
        P("blk"),
        P("blk"),
    )
    return jax.shard_map(
        body,
        mesh=mesh,
        in_specs=placed,
        out_specs=(
            P(("groups", "req"), "blk"),
            P(("groups", "req"), None, "blk", None),
            P(("groups", "req"), None, "blk", None),
        ),
        check_vma=False,
    )
```

profile of v0, /device:TPU:0, one launch (start us, length us, event | category | flops | bytes accessed | tf_op | source)
XLA Modules:
  0.0 343.2 jit_solution(14080741423998053400)
XLA Ops:
  7.2 0.0 reduce-scatter.9.cloned.1.call-start
  7.2 1.2 fusion.35
  8.4 8.4 %psum.28 = f32[80]{0:T(128)S(1)} all-reduce(f32[80]{0:T(128)S(1)} %fusion.35), channel_id=1, replica_groups=mesh['groups'=2,'blk'=4,'req'=4] {'blk'}, use_global_device_ids=true, to_apply=%region_1.0 | all-reduce | flops 80 | bytes 640 | tf_op jit(solution)/shard_map/psum | solution.py:93
  16.8 1.1 fusion.37
  18.0 7.2 %all_gather.9 = bf16[80,4608]{1,0:T(8,128)(2,1)S(1)} all-gather(bf16[80,1152]{1,0:T(8,128)(2,1)S(1)} %fusion.37), channel_id=1, replica_groups=mesh['groups'=2,'blk'=4,'req'=4] {'blk'}, dimensions={1}, use_global_device_ids=true | all-gather | bytes 921600 | tf_op jit(solution)/shard_map/all_gather | solution.py:95
  25.2 0.1 copy.94
  25.2 24.5 %all_to_all.19 = bf16[80,4,1152]{2,0,1:T(8,128)(2,1)S(1)} all-to-all(bf16[80,4,1152]{2,0,1:T(8,128)(2,1)S(1)} %bitcast.84), channel_id=1, replica_groups=mesh['groups'=2,'blk'=4,'req'=4] {'req'}, dimensions={1} | all-to-all | bytes 1474560 | tf_op jit(solution)/shard_map/all_to_all | solution.py:96
  49.8 0.6 fusion.55
  50.3 0.6 fusion.54
  51.0 1.0 fusion.53
  52.0 1.7 pad_maximum_fusion
  53.7 0.0 reduce-scatter.9.cloned.1.call-update
  53.7 0.0 reduce-scatter.13.cloned.1.call-start
  53.8 0.6 copy-done.9
  54.3 0.1 add_convert_fusion.2
  54.4 0.1 convert_element_type.72
  54.5 0.1 iota_compare_fusion
  54.6 0.2 multiply_cosine_fusion
  54.8 50.5 %reduce-scatter.9.cloned.1.call-done = f32[80,2048]{1,0:T(8,128)} async-done(((f32[320,2048]{1,0:T(8,128)}), f32[80,2048]{1,0:T(8,128)}) %reduce-scatter.9.cloned.1.call-update) | async-done | bytes 655376 | tf_op jit(solution)/shard_map/reduce_scatter | solution.py:97
  105.3 0.9 slice.46
  106.3 1.0 slice_bitcast_fusion
  107.3 0.1 copy.82
  107.4 0.9 slice.32
  108.3 0.1 reshape.148
  108.4 0.2 subtract_convert_fusion.1
  108.6 0.2 subtract_convert_fusion
  108.8 0.1 copy.57
  108.9 0.1 copy.56
  109.0 0.1 pad_maximum_fusion.2
  109.1 1.4 fusion.52
  110.5 6.0 %bitcast_reduce_fusion = (f32[16,4,2,5]{3,2,1,0:T(2,128)S(1)}, f32[16,4,5,2,512]{4,2,3,1,0:T(8,128)S(1)}) fusion(pred[16,512]{1,0:T(8,128)(4,1)S(1)} %iota_compare_fusion, bf16[16,512,4,128,1]{3,2,1,0,4:T(4,128)(2,1)} %bitcast.79, bf16[16,5,4,2,64]{4,1,3,2,0:T(8,128)(2,1)S(1)} %copy.57, bf16[16,5,4,2,64]{4,1,3,2,0:T(8,128)(2,1)S(1)} %copy.56), kind=kOutput, calls=%fused_computation.13 | convolution fusion | flops 85196160 | bytes 9873920 | tf_op jit(solution)/shard_map/rskge,rcke->rkgsc/dot_general | solution.py:39
  116.6 0.3 fusion.28
  116.8 1.0 fusion.8
  117.9 2.0 fusion.16
  119.8 0.4 fusion.22
  120.2 0.1 copy.64
  120.4 0.1 convert_element_type.76
  120.5 5.4 %fusion.5 = bf16[4608,80]{0,1:T(8,128)(2,1)S(1)} fusion(bf16[80,1024]{1,0:T(8,128)(2,1)S(1)} %convert_element_type.76, bf16[1024,4608]{1,0:T(8,128)(2,1)} %param.22), kind=kOutput, calls=%fused_computation.7 | convolution fusion | flops 755343360 | bytes 10338304 | tf_op jit(solution)/shard_map/dot_general | solution.py:134
  125.9 1.4 copy.77
  127.3 0.0 all-gather.2.cloned.1.call-start
  127.4 25.3 %reduce-scatter.13.cloned.1.call-done = bf16[1152,80]{1,0:T(8,128)(2,1)} async-done(((bf16[4608,80]{1,0:T(8,128)(2,1)}), bf16[1152,80]{1,0:T(8,128)(2,1)}) %reduce-scatter.13.cloned.1.call-update) | async-done | bytes 184336
  152.6 1.1 copy.78
  153.8 0.1 fusion.29
  153.9 5.8 %psum.29 = f32[80]{0:T(128)S(1)} all-reduce(f32[80]{0:T(128)S(1)} %fusion.29), channel_id=1, replica_groups=mesh['groups'=2,'blk'=4,'req'=4] {'blk'}, use_global_device_ids=true, to_apply=%region_9.10 | all-reduce | flops 80 | bytes 640 | tf_op jit(solution)/shard_map/psum | solution.py:144
  159.7 0.3 fusion.39
  159.9 5.7 %psum.30 = f32[80]{0:T(128)S(1)} all-reduce(f32[80]{0:T(128)S(1)} %get-tuple-element.18), channel_id=1, replica_groups=mesh['groups'=2,'blk'=4,'req'=4] {'blk'}, use_global_device_ids=true, to_apply=%region_11.12 | all-reduce | flops 80 | bytes 640 | tf_op jit(solution)/shard_map/psum | solution.py:147
  165.6 0.1 fusion.41
  165.7 8.9 %all_gather.10 = bf16[80,4608]{1,0:T(8,128)(2,1)} all-gather(bf16[80,1152]{1,0:T(8,128)(2,1)S(1)} %fusion.41), channel_id=1, replica_groups=mesh['groups'=2,'blk'=4,'req'=4] {'blk'}, dimensions={1}, use_global_device_ids=true | all-gather | bytes 921600 | tf_op jit(solution)/shard_map/all_gather | solution.py:149
  174.6 0.0 all-gather.2.cloned.1.call-update
  174.6 0.0 reduce-scatter.15.cloned.1.call-start
  174.7 60.7 %all-gather.2.cloned.1.call-done = bf16[320,4608]{1,0:T(8,128)(2,1)} async-done(((bf16[80,4608]{1,0:T(8,128)(2,1)}), bf16[320,4608]{1,0:T(8,128)(2,1)}) %all-gather.2.cloned.1.call-update) | async-done | bytes 2949136 | tf_op jit(solution)/shard_map/all_gather | solution.py:150
  235.3 9.0 %fusion.56 = f32[320,1152]{1,0:T(8,128)S(1)} fusion(bf16[320,4608]{1,0:T(8,128)(2,1)} %all-gather.2.cloned.1.call-done, bf16[1152,4608]{1,0:T(8,128)(2,1)} %param.23), kind=kOutput, calls=%fused_computation.95 | convolution fusion | flops 3397386240 | bytes 15040512 | tf_op jit(solution)/shard_map/dot_general | solution.py:151
  244.4 8.2 %fusion.6 = bf16[320,1152]{1,0:T(8,128)(2,1)S(1)} fusion(bf16[320,4608]{1,0:T(8,128)(2,1)S(1)} %copy-done.10, bf16[1152,4608]{1,0:T(8,128)(2,1)} %param.24, f32[320,1152]{1,0:T(8,128)S(1)} %fusion.56), kind=kOutput, calls=%fused_computation.9 | convolution fusion | flops 3401072640 | bytes 15777792 | tf_op jit(solution)/shard_map/dot_general | solution.py:154
  252.7 5.3 %fusion.4 = bf16[4608,320]{0,1:T(8,128)(2,1)} fusion(bf16[320,1152]{1,0:T(8,128)(2,1)S(1)} %fusion.6, bf16[1152,4608]{1,0:T(8,128)(2,1)S(1)} %bitcast.92), kind=kOutput, calls=%fused_computation.5 | convolution fusion | flops 3398860800 | bytes 14303232 | tf_op jit(solution)/shard_map/dot_general | solution.py:157
  258.0 5.5 %copy.79 = bf16[4608,320]{1,0:T(8,128)(2,1)} copy(bf16[4608,320]{0,1:T(8,128)(2,1)} %fusion.4) | data formatting | bytes 5898240
  263.5 0.0 reduce-scatter.15.cloned.1.call-update
  263.6 0.0 reduce-scatter.11.cloned.1.call-start
  263.6 39.1 %reduce-scatter.15.cloned.1.call-done = bf16[1152,320]{1,0:T(8,128)(2,1)} async-done(((bf16[4608,320]{1,0:T(8,128)(2,1)}), bf16[1152,320]{1,0:T(8,128)(2,1)}) %reduce-scatter.15.cloned.1.call-update) | async-done | bytes 737296
  302.7 2.2 copy.80
  305.0 0.7 copy.65
  305.6 22.6 %reduce-scatter.11.cloned.1.call-done = bf16[1152,80]{0,1:T(8,128)(2,1)} async-done(((bf16[1152,320]{0,1:T(8,128)(2,1)}), bf16[1152,80]{0,1:T(8,128)(2,1)}) %reduce-scatter.11.cloned.1.call-update) | async-done | bytes 184336 | tf_op jit(solution)/shard_map/reduce_scatter | solution.py:167
  328.2 1.1 fusion.32
  329.3 5.7 %psum.31 = f32[80]{0:T(128)S(1)} all-reduce(f32[80]{0:T(128)S(1)} %fusion.32), channel_id=1, replica_groups=mesh['groups'=2,'blk'=4,'req'=4] {'blk'}, use_global_device_ids=true, to_apply=%region_15.16 | all-reduce | flops 80 | bytes 640 | tf_op jit(solution)/shard_map/psum | solution.py:169
  334.9 1.7 fusion.42
  (46 shorter events, 0.3 us)
Async XLA Ops:
  7.2 43.8 %copy-start = (bf16[1152,1024]{1,0:T(8,128)(2,1)S(1)}, bf16[1152,1024]{1,0:T(8,128)(2,1)}, u32[]{:S(2)}) copy-start(bf16[1152,1024]{1,0:T(8,128)(2,1)} %param.19) | copy-start | bytes 7077892
  7.2 98.1 %reduce-scatter.9.cloned.1.call-start = ((), (), s32[]{:S(2)}) async-start(), calls=%async_computation.5 | async-start | bytes 3276800 | tf_op jit(solution)/shard_map/reduce_scatter | solution.py:97
  16.8 32.9 %copy-start.3 = (bf16[1152,512]{1,0:T(8,128)(2,1)S(1)}, bf16[1152,512]{1,0:T(8,128)(2,1)}, u32[]{:S(2)}) copy-start(bf16[1152,512]{1,0:T(8,128)(2,1)} %param.21) | copy-start | bytes 3538948
  25.2 25.1 %copy-start.4 = (bf16[1152,512]{1,0:T(8,128)(2,1)S(1)}, bf16[1152,512]{1,0:T(8,128)(2,1)}, u32[]{:S(2)}) copy-start(bf16[1152,512]{1,0:T(8,128)(2,1)} %param.20) | copy-start | bytes 3538948
  53.7 0.7 copy-start.9
  53.7 98.9 %reduce-scatter.13.cloned.1.call-start = ((), (), s32[]{:S(2)}) async-start(), calls=%async_computation.8 | async-start | bytes 1474560
  106.3 13.6 %copy-start.5 = (bf16[16,5,4,128]{3,2,1,0:T(4,128)(2,1)}, bf16[16,5,4,128]{3,2,1,0:T(4,128)(2,1)S(1)}, u32[]{:S(2)}) copy-start(bf16[16,5,4,128]{3,2,1,0:T(4,128)(2,1)S(1)} %reshape.149) | copy-start | bytes 245764
  109.1 8.8 %slice-start.3 = ((s8[8388608]{0:T(1024)(128)(4,1)}), s8[4194304]{0:T(1024)(128)(4,1)S(1)}, s32[]{:S(2)}) async-start(s8[8388608]{0:T(1024)(128)(4,1)} %bitcast.93), calls=%async_computation.13 | async-start | bytes 8388608
  110.5 7.4 %slice-start.4 = ((s8[8388608]{0:T(1024)(128)(4,1)}), s8[4194304]{0:T(1024)(128)(4,1)S(1)}, s32[]{:S(2)}) async-start(s8[8388608]{0:T(1024)(128)(4,1)} %bitcast.93), calls=%async_computation.14 | async-start | bytes 8388608
  125.9 33.8 %copy-start.2 = (bf16[80,1152]{1,0:T(8,128)(2,1)S(1)}, bf16[80,1152]{1,0:T(8,128)(2,1)}, u32[]{:S(2)}) copy-start(bf16[80,1152]{1,0:T(8,128)(2,1)} %param.15) | copy-start | bytes 552964
  125.9 33.8 %copy-start.6 = (f32[1152]{0:T(1024)S(1)}, f32[1152]{0:T(1024)}, u32[]{:S(2)}) copy-start(f32[1152]{0:T(1024)} %param.27) | copy-start | bytes 13828
  125.9 39.7 %copy-start.8 = (f32[1152]{0:T(1024)S(1)}, f32[1152]{0:T(1024)}, u32[]{:S(2)}) copy-start(f32[1152]{0:T(1024)} %param.28) | copy-start | bytes 13828
  127.3 108.0 %all-gather.2.cloned.1.call-start = ((), (), s32[]{:S(2)}) async-start(), calls=%async_computation.6 | async-start | bytes 3686400 | tf_op jit(solution)/shard_map/all_gather | solution.py:150
  174.6 128.1 %reduce-scatter.15.cloned.1.call-start = ((), (), s32[]{:S(2)}) async-start(), calls=%async_computation.9 | async-start | bytes 4423680
  235.3 9.0 %copy-start.10 = (bf16[320,4608]{1,0:T(8,128)(2,1)S(1)}, bf16[320,4608]{1,0:T(8,128)(2,1)}, u32[]{:S(2)}) copy-start(bf16[320,4608]{1,0:T(8,128)(2,1)} %all-gather.2.cloned.1.call-done) | copy-start | bytes 8847364
  235.3 17.3 %slice-start = ((s8[10616832]{0:T(1024)(128)(4,1)}), s8[4194304]{0:T(1024)(128)(4,1)S(1)}, s32[]{:S(2)}) async-start(s8[10616832]{0:T(1024)(128)(4,1)} %bitcast.91), calls=%async_computation.10 | async-start | bytes 8388608
  235.3 17.3 %slice-start.1 = ((s8[10616832]{0:T(1024)(128)(4,1)}), s8[4194304]{0:T(1024)(128)(4,1)S(1)}, s32[]{:S(2)}) async-start(s8[10616832]{0:T(1024)(128)(4,1)} %bitcast.91), calls=%async_computation.11 | async-start | bytes 8388608
  244.4 8.3 %slice-start.2 = ((s8[10616832]{0:T(1024)(128)(4,1)}), s8[2228224]{0:T(1024)(128)(4,1)S(1)}, s32[]{:S(2)}) async-start(s8[10616832]{0:T(1024)(128)(4,1)} %bitcast.91), calls=%async_computation.12 | async-start | bytes 4456448
  263.6 71.4 %copy-start.7 = (f32[1152]{0:T(1024)S(1)}, f32[1152]{0:T(1024)}, u32[]{:S(2)}) copy-start(f32[1152]{0:T(1024)} %param.29) | copy-start | bytes 13828
  263.6 73.1 %copy-start.1 = (bf16[1152,1024]{1,0:T(8,128)(2,1)S(1)}, bf16[1152,1024]{1,0:T(8,128)(2,1)}, u32[]{:S(2)}) copy-start(bf16[1152,1024]{1,0:T(8,128)(2,1)} %param.19) | copy-start | bytes 7077892
  263.6 64.6 %reduce-scatter.11.cloned.1.call-start = ((), (), s32[]{:S(2)}) async-start(), calls=%async_computation.7 | async-start | bytes 921600 | tf_op jit(solution)/shard_map/reduce_scatter | solution.py:167
Sparse Core Ops, SparseCore 0:
  53.8 51.4 reduce-scatter.8
  127.4 25.1 reduce-scatter.12
  174.7 60.5 all-gather.1
  263.7 39.0 reduce-scatter.14
  305.1 23.0 reduce-scatter.10
where the time goes:
time: 344 us; the launch traced here: 343 us
  waiting for transfers between devices  198 us (58%)
  blocking collectives  66 us (19%)
  matrix products  39.9 us (12%)
  local copies, waits for them, and re-layouts  15.1 us (4%)
  between operations  14.2 us (4%)
  other arithmetic  9.58 us (3%)
    unnamed x7, waiting for transfers between devices  64.5 us
    all_gather x1, waiting for transfers between devices, body(): piece = lax.all_gather(features, 'req', axis=0, tiled=True)  60.7 us
    reduce_scatter x1, waiting for transfers between devices, body(): lax.psum_scatter(jnp.concatenate([jnp.dot(slices, q_weight, preferred_ele...  50.5 us
    all_to_all x1, blocking collectives, body(): lax.all_to_all(whole, 'req', split_axis=1, concat_axis=0, tiled=True)  24.5 us
    reduce_scatter x1, waiting for transfers between devices, body(): lax.psum_scatter(partial_sum, 'req', scatter_dimension=1, tiled=True)  22.6 us
    unnamed x39, local copies, waits for them, and re-layouts  12.6 us
    dot_general x1, matrix products, body(): lax.dot_general(piece, gate_weight, (((1,), (1,)), ((), ())), preferred_e...  9.03 us
    all_gather x1, blocking collectives, body(): features = lax.all_gather(normed_mid, 'blk', axis=1, tiled=True)  8.85 us
  transfers between devices with their start and end apart: 5, of which 5 were waited for; matrix products, arithmetic and copies ran while one was open for 0% of the time, Pallas kernels for 0%

commit v1 on v0

v1 whole, which is shorter than its diff:
```python
import functools

import jax
import jax.numpy as jnp
from jax import lax
from jax.experimental import pallas as pl
from jax.experimental.pallas import tpu as pltpu
from jax.sharding import PartitionSpec as P

D = 4608
HEADS = 32


EPSILON = 1e-06
NEGATIVE = -1e30


def rotate(values, positions):
    size = values.shape[-1]
    half = size // 2
    rates = 10000.0 ** (-(jnp.arange(half, dtype=jnp.float32) * 2.0) / size)
    angle = positions.astype(jnp.float32)[..., None] * rates
    cosine = jnp.cos(angle)
    sine = jnp.sin(angle)
    first = values[..., :half]
    second = values[..., half:]
    return jnp.concatenate(
        [first * cosine - second * sine, second * cosine + first * sine], axis=-1
    )


def scaling(total):
    return lax.rsqrt(total / D + EPSILON)[:, None]


def attend(queries, new_keys, new_values, cache_keys, cache_values, lengths):
    req_count, steps, heads, size = queries.shape
    shared = new_keys.shape[2]
    group = heads // shared
    scale = (D // HEADS) ** (-0.5)
    grouped = queries.reshape(req_count, steps, shared, group, size)
    older = (
        jnp.einsum("rskge,rcke->rkgsc", grouped, cache_keys, preferred_element_type=jnp.float32)
        * scale
    )
    newer = (
        jnp.einsum("rskge,rtke->rkgst", grouped, new_keys, preferred_element_type=jnp.float32)
        * scale
    )
    valid = jnp.arange(cache_keys.shape[1], dtype=jnp.int32)[None, :] < lengths[:, None]
    older = jnp.where(valid[:, None, None, None, :], older, NEGATIVE)
    causal = (
        jnp.arange(steps, dtype=jnp.int32)[:, None] >= jnp.arange(steps, dtype=jnp.int32)[None, :]
    )
    newer = jnp.where(causal, newer, NEGATIVE)
    highest = jnp.maximum(jnp.max(older, axis=-1), jnp.max(newer, axis=-1))[..., None]
    far_mass = jnp.exp(older - highest)
    near_mass = jnp.exp(newer - highest)
    total_mass = (jnp.sum(far_mass, axis=-1) + jnp.sum(near_mass, axis=-1))[..., None]
    far_weights = (far_mass / total_mass).astype(jnp.bfloat16)
    near_weights = (near_mass / total_mass).astype(jnp.bfloat16)
    blended = jnp.einsum(
        "rkgsc,rcke->rskge", far_weights, cache_values, preferred_element_type=jnp.float32
    )
    blended = blended + jnp.einsum(
        "rkgst,rtke->rskge", near_weights, new_values, preferred_element_type=jnp.float32
    )
    return blended.reshape(req_count * steps, heads * size).astype(jnp.bfloat16)


LANES = 128
BF = jnp.bfloat16
F32 = jnp.float32
DMA = pltpu.SemaphoreType.DMA


def remote(src, dst, send_sem, recv_sem, **device):
    return pltpu.make_async_remote_copy(
        src_ref=src,
        dst_ref=dst,
        send_sem=send_sem,
        recv_sem=recv_sem,
        device_id=device,
        device_id_type=pl.DeviceIdType.MESH,
    )


def greet(blks, reqs):
    b, r = lax.axis_index("blk"), lax.axis_index("req")
    barrier = pltpu.get_barrier_semaphore()
    for k in range(1, blks):
        pl.semaphore_signal(
            barrier,
            inc=1,
            device_id={"blk": lax.rem(b + k, blks)},
            device_id_type=pl.DeviceIdType.MESH,
        )
    for k in range(1, reqs):
        pl.semaphore_signal(
            barrier,
            inc=1,
            device_id={"req": lax.rem(r + k, reqs)},
            device_id_type=pl.DeviceIdType.MESH,
        )
    pl.semaphore_wait(barrier, blks + reqs - 2)
    return b, r


def diagonal(rows):
    return lax.broadcasted_iota(jnp.int32, (rows, LANES), 0) == lax.broadcasted_iota(
        jnp.int32, (rows, LANES), 1
    )


def send_sums(values, buf, send_sem, recv_sem, b, blks):
    rows = values.shape[0]
    packed = jnp.sum(jnp.where(diagonal(rows), values, 0.0), axis=0, keepdims=True)
    buf[b] = jnp.broadcast_to(packed, (8, LANES))
    for k in range(1, blks):
        remote(
            buf.at[b], buf.at[b], send_sem.at[k], recv_sem.at[k], blk=lax.rem(b + k, blks)
        ).start()


def take_sums(rows, buf, send_sem, recv_sem, b, blks):
    for k in range(1, blks):
        src = lax.rem(b + blks - k, blks)
        remote(buf.at[src], buf.at[src], send_sem.at[k], recv_sem.at[k], blk=src).wait_recv()
    total = buf[0]
    for j in range(1, blks):
        total = total + buf[j]
    for k in range(1, blks):
        src = lax.rem(b + blks - k, blks)
        remote(buf.at[b], buf.at[b], send_sem.at[k], recv_sem.at[k], blk=src).wait_send()
    spread = jnp.where(diagonal(rows), total[0:1, :], 0.0)
    return jnp.sum(spread, axis=1, keepdims=True)


def inverse(total):
    return lax.rsqrt(total / D + EPSILON)


def gather_kernel(
    blks, reqs, x_ref, gain_ref, out, scale_ref, ybuf, sums, ss, sr, s0, zsend, recv, psend, xsend
):
    b, r = greet(blks, reqs)
    per = blks // reqs
    chips = blks // 2
    x, c = b // 2, lax.rem(b, 2)
    mate = b + 1 - 2 * c
    other = lax.rem(b + 2, blks) if chips > 1 else mate
    home = b // per
    mine = lax.rem(b, per)
    states = x_ref[...].astype(F32)
    ybuf[...] = (states * gain_ref[...]).astype(BF)

    @pl.when(r != home)
    def _():
        remote(ybuf, out.at[mine, r], zsend, recv.at[mine, r], req=home).start()

    @pl.when(r == home)
    def _():
        copy = pltpu.make_async_copy(ybuf, out.at[mine, r], s0)
        copy.start()
        copy.wait()

    send_sums(jnp.sum(states * states, axis=1, keepdims=True), sums, ss, sr, b, blks)

    def visit(j, rp):
        owner = r * per + j
        slot = out.at[j, rp]

        @pl.when(jnp.logical_or(b != owner, rp != r))
        def _():
            remote(slot, slot, psend.at[j, rp], recv.at[j, rp], blk=mate).wait_recv()

        @pl.when(lax.rem(owner, 2) == c)
        def _():
            remote(slot, slot, psend.at[j, rp], recv.at[j, rp], blk=mate).start()

        @pl.when(b == owner)
        def _():
            for k in range(1, chips):
                remote(
                    slot,
                    slot,
                    xsend.at[k, rp],
                    recv.at[j, rp],
                    blk=lax.rem(b + 2 * k, blks),
                ).start()

    def finish(j, rp):
        owner = r * per + j
        slot = out.at[j, rp]

        @pl.when(lax.rem(owner, 2) == c)
        def _():
            remote(slot, slot, psend.at[j, rp], recv.at[j, rp], blk=mate).wait_send()

        @pl.when(b == owner)
        def _():
            for k in range(1, chips):
                remote(slot, slot, xsend.at[k, rp], recv.at[j, rp], blk=other).wait_send()

    for call in (visit, finish):
        for dist in range(reqs):
            for rp in (r + dist, r - dist) if dist else (r,):

                @pl.when(jnp.logical_and(rp >= 0, rp < reqs))
                def _(rp=rp):
                    for j in range(per):
                        call(j, rp)

    @pl.when(r != home)
    def _():
        remote(ybuf, out.at[mine, r], zsend, recv.at[mine, r], req=home).wait_send()

    total = take_sums(x_ref.shape[0], sums, ss, sr, b, blks)
    scale_ref[...] = jnp.broadcast_to(inverse(total), scale_ref.shape)


def chain_step(reqs, r, d, part, left, right, lsend, lrecv, rsend, rrecv):
    def step(go, first, buf, send_sem, recv_sem, nxt):
        @pl.when(go)
        def _():
            @pl.when(first)
            def _():
                remote(part.at[d], buf.at[d], send_sem.at[d], recv_sem.at[d], req=nxt).start()

            @pl.when(jnp.logical_not(first))
            def _():
                remote(part.at[d], buf.at[d], send_sem.at[d], recv_sem.at[d], req=nxt).wait_recv()
                buf[d] = (buf[d].astype(F32) + part[d].astype(F32)).astype(BF)
                remote(buf.at[d], buf.at[d], send_sem.at[d], recv_sem.at[d], req=nxt).start()

    step(r < d, r == 0, left, lsend, lrecv, r + 1)
    step(r > d, r == reqs - 1, right, rsend, rrecv, r - 1)


def chain_order(reqs):
    order = []
    for k in range(reqs):
        order.append(reqs - 1 - k // 2 if k % 2 == 0 else k // 2)
    return order


def chain_end(reqs, r, part, left, right, lsend, lrecv, rsend, rrecv, total):
    total[...] = part[r].astype(F32)

    @pl.when(r > 0)
    def _():
        remote(left.at[r], left.at[r], lsend.at[r], lrecv.at[r], req=r - 1).wait_recv()
        total[...] += left[r].astype(F32)

    @pl.when(r < reqs - 1)
    def _():
        remote(right.at[r], right.at[r], rsend.at[r], rrecv.at[r], req=r + 1).wait_recv()
        total[...] += right[r].astype(F32)

    for d in range(reqs):

        @pl.when(r < d)
        def _():
            remote(left.at[d], left.at[d], lsend.at[d], lrecv.at[d], req=r + 1).wait_send()

        @pl.when(r > d)
        def _():
            remote(right.at[d], right.at[d], rsend.at[d], rrecv.at[d], req=r - 1).wait_send()


def project_kernel(
    blks, reqs, part, scale_ref, out, left, right, lsend, lrecv, rsend, rrecv
):
    b, r = greet(blks, reqs)
    for d in chain_order(reqs):
        chain_step(reqs, r, d, part, left, right, lsend, lrecv, rsend, rrecv)
    chain_end(reqs, r, part, left, right, lsend, lrecv, rsend, rrecv, out)
    out[...] = out[...] * scale_ref[:, 0:1]


def view(ref, blk, rows=None):
    if len(ref.shape) == 2:
        width = D // lax.axis_size("blk")
        cols = pl.ds(pl.multiple_of(blk * width, LANES), width)
        if rows is None:
            return ref.at[:, cols]
        height = ref.shape[0] // lax.axis_size("req")
        return ref.at[pl.ds(pl.multiple_of(rows * height, 16), height), cols]
    return ref.at[blk] if rows is None else ref.at[blk, rows]


def middle_kernel(
    blks, reqs, part, x_ref, post_ref, gain_ref, full, mid_ref,
    rp, rx, own, sums1, sums2, psend0, precv0, xsend0, xrecv0, ss1, sr1, ss2, sr2,
    s0, zsend, recv, psend, xsend,
):
    b, r = greet(blks, reqs)
    chips = blks // 2
    x, c = b // 2, lax.rem(b, 2)
    mate = b + 1 - 2 * c
    rows = x_ref.shape[0]
    for k in list(range(1, chips)) + [0]:
        xp = lax.rem(x + k, chips)
        remote(
            view(part, 2 * xp + 1 - c), rp.at[xp], psend0.at[k], precv0.at[k], blk=mate
        ).start()
    for k in range(1, chips):
        xp = lax.rem(x + k, chips)
        remote(rp.at[xp], rp.at[xp], psend0.at[k], precv0.at[k], blk=mate).wait_recv()
        rp[xp] = (rp[xp].astype(F32) + view(part, 2 * xp + c)[...].astype(F32)).astype(BF)
        remote(rp.at[xp], rx.at[k], xsend0.at[k], xrecv0.at[k], blk=2 * xp + c).start()
    remote(rp.at[x], rp.at[x], psend0.at[0], precv0.at[0], blk=mate).wait_recv()
    mixed = view(part, b)[...].astype(F32) + rp[x].astype(F32)
    for k in range(1, chips):
        xp = lax.rem(x + k, chips)
        remote(rx.at[k], rx.at[k], xsend0.at[k], xrecv0.at[k], blk=2 * xp + c).wait_recv()
        mixed = mixed + rx[k].astype(F32)
    send_sums(jnp.sum(mixed * mixed, axis=1, keepdims=True), sums1, ss1, sr1, b, blks)
    total = take_sums(rows, sums1, ss1, sr1, b, blks)
    middle = (x_ref[...].astype(F32) + mixed * inverse(total) * post_ref[...]).astype(BF)
    mid_ref[...] = middle
    wide = middle.astype(F32)
    send_sums(jnp.sum(wide * wide, axis=1, keepdims=True), sums2, ss2, sr2, b, blks)
    total = take_sums(rows, sums2, ss2, sr2, b, blks)
    own[...] = (wide * inverse(total) * gain_ref[...]).astype(BF)
    copy = pltpu.make_async_copy(own, view(full, b, r), s0)
    copy.start()

    def spread(rp_, src, go):
        dst = view(full, b, rp_)
        if go >= 0:

            @pl.when(r + 1 < reqs)
            def _():
                remote(src, dst, zsend.at[0, rp_], recv.at[b, rp_], req=r + 1).start()

        if go <= 0:

            @pl.when(r > 0)
            def _():
                remote(src, dst, zsend.at[1, rp_], recv.at[b, rp_], req=r - 1).start()

        for k in range(1, chips):
            to = lax.rem(b + 2 * k, blks)
            remote(src, dst, xsend.at[k, rp_], recv.at[b, rp_], blk=to).start()
        remote(src, dst, psend.at[x, rp_], recv.at[b, rp_], blk=mate).start()

    def arrive(owner, rp_):
        slot = view(full, owner, rp_)
        remote(slot, slot, psend.at[0, rp_], recv.at[owner, rp_], blk=mate).wait_recv()

    def relay(rp_):
        for k in range(1, chips):
            xp = lax.rem(x + k, chips)
            owner = 2 * xp + c
            arrive(owner, rp_)
            slot = view(full, owner, rp_)
            remote(slot, slot, psend.at[xp, rp_], recv.at[owner, rp_], blk=mate).start()

    def within(rp_, call):
        @pl.when(jnp.logical_and(rp_ >= 0, rp_ < reqs))
        def _():
            call()

    spread(r, own, 0)
    for dist in range(1, reqs):

        def up():
            arrive(b, r - dist)
            spread(r - dist, view(full, b, r - dist), 1)

        def down():
            arrive(b, r + dist)
            spread(r + dist, view(full, b, r + dist), -1)

        within(r - dist, up)
        within(r + dist, down)
        if dist == 1:
            relay(r)
        else:
            within(r - dist + 1, lambda: relay(r - dist + 1))
            within(r + dist - 1, lambda: relay(r + dist - 1))
    within(r - reqs + 1, lambda: relay(r - reqs + 1))
    within(r + reqs - 1, lambda: relay(r + reqs - 1))
    copy.wait()
    for xp in range(chips):
        for d in range(reqs):
            arrive(2 * xp + 1 - c, d)
    for d in range(reqs):
        slot = view(full, b, d)

        @pl.when(jnp.logical_and(d <= r, r + 1 < reqs))
        def _():
            remote(slot, slot, zsend.at[0, d], recv.at[b, d], blk=mate).wait_send()

        @pl.when(jnp.logical_and(d >= r, r > 0))
        def _():
            remote(slot, slot, zsend.at[1, d], recv.at[b, d], blk=mate).wait_send()

        for k in range(1, chips):
            remote(slot, slot, xsend.at[k, d], recv.at[b, d], blk=mate).wait_send()
        for xp in range(chips):
            remote(slot, slot, psend.at[xp, d], recv.at[b, d], blk=mate).wait_send()
    for k in range(chips):
        remote(rp.at[0], rp.at[0], psend0.at[k], precv0.at[k], blk=mate).wait_send()
    for k in range(1, chips):
        remote(rp.at[0], rp.at[0], xsend0.at[k], xrecv0.at[k], blk=mate).wait_send()


def last_kernel(
    blks, reqs, part, mid_ref, post_ref, out,
    rp, rx, own, left, right, acc, sums, psend, precv, xsend, xrecv,
    lsend, lrecv, rsend, rrecv, ss, sr,
):
    b, r = greet(blks, reqs)
    chips = blks // 2
    x, c = b // 2, lax.rem(b, 2)
    mate = b + 1 - 2 * c
    rows = mid_ref.shape[0]
    order = chain_order(reqs)
    for d in order:
        for k in list(range(1, chips)) + [0]:
            xp = lax.rem(x + k, chips)
            remote(
                view(part, 2 * xp + 1 - c, d), rp.at[xp, d], psend.at[k, d], precv.at[k, d], blk=mate
            ).start()
    for d in order:
        for k in range(1, chips):
            xp = lax.rem(x + k, chips)
            slot = rp.at[xp, d]
            remote(slot, slot, psend.at[k, d], precv.at[k, d], blk=mate).wait_recv()
            rp[xp, d] = (rp[xp, d].astype(F32) + view(part, 2 * xp + c, d)[...].astype(F32)).astype(BF)
            remote(slot, rx.at[k, d], xsend.at[k, d], xrecv.at[k, d], blk=2 * xp + c).start()
    for d in order:
        slot = rp.at[x, d]
        remote(slot, slot, psend.at[0, d], precv.at[0, d], blk=mate).wait_recv()
        value = view(part, b, d)[...].astype(F32) + rp[x, d].astype(F32)
        for k in range(1, chips):
            slot = rx.at[k, d]
            remote(slot, slot, xsend.at[k, d], xrecv.at[k, d], blk=mate).wait_recv()
            value = value + rx[k, d].astype(F32)
        own[d] = value.astype(BF)
        chain_step(reqs, r, d, own, left, right, lsend, lrecv, rsend, rrecv)
    chain_end(reqs, r, own, left, right, lsend, lrecv, rsend, rrecv, acc)
    ffn = acc[...]
    send_sums(jnp.sum(ffn * ffn, axis=1, keepdims=True), sums, ss, sr, b, blks)
    for d in range(reqs):
        for k in range(chips):
            slot = rp.at[0, d]
            remote(slot, slot, psend.at[k, d], precv.at[k, d], blk=mate).wait_send()
            if k:
                remote(slot, slot, xsend.at[k, d], xrecv.at[k, d], blk=mate).wait_send()
    total = take_sums(rows, sums, ss, sr, b, blks)
    out[...] = (mid_ref[...].astype(F32) + ffn * inverse(total) * post_ref[...]).astype(BF)


def call(kernel, sizes, number, outs, scratch, *args):
    vmem = pl.BlockSpec(memory_space=pltpu.VMEM)
    return pl.pallas_call(
        functools.partial(kernel, *sizes),
        out_shape=outs,
        in_specs=[vmem] * len(args),
        out_specs=jax.tree.map(lambda _: vmem, outs),
        scratch_shapes=scratch,
        compiler_params=pltpu.CompilerParams(
            collective_id=number, has_side_effects=True, vmem_limit_bytes=40 * 2**20
        ),
    )(*args)


def body(
    hidden_states,
    context_lengths,
    cache_keys,
    cache_values,
    q_weight,
    k_weight,
    v_weight,
    o_weight,
    gate_weight,
    up_weight,
    down_weight,
    attn_gain,
    post_attn_gain,
    ffn_gain,
    post_ffn_gain,
):
    blks, reqs = lax.axis_size("blk"), lax.axis_size("req")
    sizes = (blks, reqs)
    per, chips = blks // reqs, blks // 2
    rows, width = hidden_states.shape
    assert blks % reqs == 0 and blks % 2 == 0 and rows <= LANES
    req_count = context_lengths.shape[0]
    steps = rows // req_count
    kv_local = cache_keys.shape[2]
    size = cache_keys.shape[3]
    query_cols = q_weight.shape[1]
    key_cols = k_weight.shape[1]
    heads_local = query_cols // size
    shape = jax.ShapeDtypeStruct
    sums = pltpu.VMEM((blks, 8, LANES), F32)
    gathered, scale = call(
        gather_kernel,
        sizes,
        0,
        (shape((per, reqs, rows, width), BF), shape((rows, LANES), F32)),
        [
            pltpu.VMEM((rows, width), BF),
            sums,
            DMA((blks,)),
            DMA((blks,)),
            DMA,
            DMA,
            DMA((per, reqs)),
            DMA((per, reqs)),
            DMA((chips, reqs)),
        ],
        hidden_states,
        attn_gain[None, :],
    )
    slices = gathered.transpose(1, 2, 0, 3).reshape(reqs * rows, per * width)
    parts = jnp.concatenate(
        [
            jnp.dot(slices, weight, preferred_element_type=F32).astype(BF)
            for weight in (q_weight, k_weight, v_weight)
        ],
        axis=1,
    )
    cols = parts.shape[1]
    joined = call(
        project_kernel,
        sizes,
        1,
        shape((rows, cols), F32),
        [pltpu.VMEM((reqs, rows, cols), BF)] * 2 + [DMA((reqs,))] * 4,
        parts.reshape(reqs, rows, cols),
        scale,
    )
    query_lin = joined[:, :query_cols]
    key_lin = joined[:, query_cols : query_cols + key_cols]
    value_lin = joined[:, query_cols + key_cols :]
    positions = (context_lengths[:, None] + jnp.arange(steps, dtype=jnp.int32)[None, :]).reshape(
        rows
    )
    queries = rotate(query_lin.reshape(rows, heads_local, size), positions[:, None]).astype(BF)
    new_keys = rotate(key_lin.reshape(rows, kv_local, size), positions[:, None]).astype(BF)
    draft_keys = new_keys.reshape(req_count, steps, kv_local, size)
    draft_values = value_lin.astype(BF).reshape(req_count, steps, kv_local, size)
    attended = attend(
        queries.reshape(req_count, steps, heads_local, size),
        draft_keys,
        draft_values,
        cache_keys,
        cache_values,
        context_lengths,
    )
    mixed = jnp.dot(attended, o_weight, preferred_element_type=F32).astype(BF)
    flat = width % LANES == 0 and rows % 16 == 0
    if not flat:
        mixed = mixed.reshape(rows, blks, width).transpose(1, 0, 2)
    full, middle = call(
        middle_kernel,
        sizes,
        2,
        (
            shape((reqs * rows, D) if flat else (blks, reqs, rows, width), BF),
            shape((rows, width), BF),
        ),
        [
            pltpu.VMEM((chips, rows, width), BF),
            pltpu.VMEM((chips, rows, width), BF),
            pltpu.VMEM((rows, width), BF),
            sums,
            sums,
        ]
        + [DMA((chips,))] * 4
        + [DMA((blks,))] * 4
        + [DMA, DMA((2, reqs)), DMA((blks, reqs)), DMA((chips, reqs)), DMA((chips, reqs))],
        mixed,
        hidden_states,
        post_attn_gain[None, :],
        ffn_gain[None, :],
    )
    if not flat:
        full = full.transpose(1, 2, 0, 3).reshape(reqs * rows, D)
    gate = lax.dot_general(full, gate_weight, (((1,), (1,)), ((), ())), preferred_element_type=F32)
    up = lax.dot_general(full, up_weight, (((1,), (1,)), ((), ())), preferred_element_type=F32)
    hidden = (jax.nn.gelu(gate, approximate=True) * up).astype(BF)
    terms = jnp.dot(hidden, down_weight, preferred_element_type=F32).astype(BF)
    if not flat:
        terms = terms.reshape(reqs, rows, blks, width).transpose(2, 0, 1, 3)
    layer_output = call(
        last_kernel,
        sizes,
        3,
        shape((rows, width), BF),
        [pltpu.VMEM((chips, reqs, rows, width), BF)] * 2
        + [pltpu.VMEM((reqs, rows, width), BF)] * 3
        + [pltpu.VMEM((rows, width), F32), sums]
        + [DMA((chips, reqs))] * 4
        + [DMA((reqs,))] * 4
        + [DMA((blks,))] * 2,
        terms,
        middle,
        post_ffn_gain[None, :],
    )
    return (layer_output, draft_keys, draft_values)


def solution(mesh):
    placed = (
        P(("groups", "req"), "blk"),
        P(("groups", "req")),
        P(("groups", "req"), None, "blk", None),
        P(("groups", "req"), None, "blk", None),
        P("req", "blk"),
        P("req", "blk"),
        P("req", "blk"),
        P("blk", None),
        P(("blk", "req"), None),
        P(("blk", "req"), None),
        P(("blk", "req"), None),
        P("blk"),
        P("blk"),
        P("blk"),
        P("blk"),
    )
    return jax.shard_map(
        body,
        mesh=mesh,
        in_specs=placed,
        out_specs=(
            P(("groups", "req"), "blk"),
            P(("groups", "req"), None, "blk", None),
            P(("groups", "req"), None, "blk", None),
        ),
        check_vma=False,
    )
```

time: 344 us -> 176 us (0.51)
  waiting for transfers between devices: 198 us -> 0 us
  Pallas kernels: 0 us -> 125 us
  blocking collectives: 66 us -> 0 us
  between operations: 14.2 us -> 1.04 us
  local copies, waits for them, and re-layouts: 15.1 us -> 5.96 us
  other arithmetic: 9.58 us -> 3.67 us
    pallas_call x0 -> x4, Pallas kernels: none -> 125 us  [call(): pl.pallas_call(functools.partial(kernel, *sizes), out_shape=outs, in_spec...]
    reduce_scatter x2 -> x0, waiting for transfers between devices: 73 us -> none  [the longest x1 50.5 us: body(): lax.psum_scatter(jnp.concatenate([jnp.dot(slices, q_weight, preferred_ele...]
    unnamed x7 -> x0, waiting for transfers between devices: 64.5 us -> none
    all_gather x1 -> x0, waiting for transfers between devices: 60.7 us -> none  [body(): piece = lax.all_gather(features, 'req', axis=0, tiled=True)]
    psum x4 -> x0, blocking collectives: 25.5 us -> none  [the longest x1 8.37 us: body(): total = lax.psum(jnp.sum(states * states, axis=1), 'blk')]
    all_to_all x1 -> x0, blocking collectives: 24.5 us -> none  [body(): lax.all_to_all(whole, 'req', split_axis=1, concat_axis=0, tiled=True)]
    all_gather x2 -> x0, blocking collectives: 16.1 us -> none  [the longest x1 8.85 us: body(): features = lax.all_gather(normed_mid, 'blk', axis=1, tiled=True)]
    unnamed x39 -> x26, local copies, waits for them, and re-layouts: 12.6 us -> 2.42 us
  transfers between devices with their start and end apart: 5 -> 0, of which waited for: 5 -> 0; matrix products, arithmetic and copies ran while one was open for 0% -> 0% of each run, Pallas kernels for 0% -> 0%
where the time goes in v1:
time: 176 us; the launch traced here: 174 us
  Pallas kernels  125 us (71%)
  matrix products  38.4 us (22%)
  local copies, waits for them, and re-layouts  5.96 us (3%)
  other arithmetic  3.67 us (2%)
    pallas_call x4, Pallas kernels, call(): pl.pallas_call(functools.partial(kernel, *sizes), out_shape=outs, in_spec...  125 us
    dot_general x1, matrix products, body(): terms = jnp.dot(hidden, down_weight, preferred_element_type=F32).astype(BF)  8.62 us
    dot_general x1, matrix products, body(): lax.dot_general(full, gate_weight, (((1,), (1,)), ((), ())), preferred_el...  6.89 us
    dot_general x1, matrix products, attend(): jnp.einsum('rskge,rcke->rkgsc', grouped, cache_keys, preferred_element_ty...  6.02 us
    dot_general x1, matrix products, body(): mixed = jnp.dot(attended, o_weight, preferred_element_type=F32).astype(BF)  5.58 us
    dot_general x1, matrix products, body(): lax.dot_general(full, up_weight, (((1,), (1,)), ((), ())), preferred_elem...  4.05 us

profile of v1, /device:TPU:0, one launch (start us, length us, event | category | flops | bytes accessed | tf_op | source)
XLA Modules:
  0.0 173.6 jit_solution(15743805937176838051)
XLA Ops:
  0.6 0.0 copy-start
  0.7 0.9 broadcast_in_dim.46.gain_ref
  1.5 0.7 broadcast_in_dim.50.post_ref
  2.2 0.7 broadcast_in_dim.51.gain_ref
  2.9 0.7 broadcast_in_dim.52.post_ref
  3.6 0.7 iota_compare_fusion
  4.4 0.7 add_convert_fusion.2
  5.1 0.1 convert_element_type.52
  5.2 0.2 multiply_cosine_fusion
  5.4 0.0 copy-start.2
  5.4 0.9 copy-done.2
  6.3 0.0 copy-start.5
  6.3 19.8 %shard_map.166 = (bf16[1,4,80,1152]{3,2,1,0:T(8,128)(2,1)S(1)}, f32[80,128]{1,0:T(8,128)S(1)}) custom-call(bf16[80,1152]{1,0:T(8,128)(2,1)S(1)} %copy-done.2, f32[1,1152]{1,0:T(1,128)S(1)} %broadcast_in_dim.46.gain_ref), custom_call_target="tpu_custom_call" | custom-call | tf_op jit(solution)/shard_map/pallas_call | solution.py:459
  26.2 1.9 %convolution_convert_fusion.3 = bf16[320,512]{1,0:T(8,128)(2,1)S(1)} fusion(bf16[320,1152]{1,0:T(8,128)(2,1)S(1)} %bitcast.56, bf16[1152,512]{1,0:T(8,128)(2,1)} %param.21), kind=kOutput, calls=%fused_computation.30 | convolution fusion | flops 377651200 | bytes 2244608 | tf_op jit(solution)/shard_map/dot_general | solution.py:524
  28.0 0.0 copy-done.5
  28.0 0.6 convolution_convert_fusion.4
  28.6 0.0 copy-done
  28.6 1.0 convolution_convert_fusion.2
  29.7 0.1 pad_maximum_fusion
  29.8 36.2 %shard_map.167 = f32[80,2048]{1,0:T(8,128)S(1)} custom-call(bf16[4,80,2048]{2,1,0:T(8,128)(2,1)S(1)} %bitcast.55, f32[80,128]{1,0:T(8,128)S(1)} %get-tuple-element.8.scale_ref), custom_call_target="tpu_custom_call" | custom-call | tf_op jit(solution)/shard_map/pallas_call | solution.py:459
  66.1 0.0 copy-start.4
  66.2 0.1 copy.44
  66.3 0.1 reshape.141
  66.3 0.2 subtract_convert_fusion.1
  66.5 0.2 subtract_convert_fusion
  66.8 0.1 pad_maximum_fusion.2
  66.9 0.7 copy.32
  67.6 0.1 copy.24
  67.7 0.1 copy.23
  67.7 0.0 slice-start.3
  67.7 1.4 fusion.35
  69.1 0.0 slice-start.4
  69.1 6.0 %bitcast_reduce_fusion = (f32[16,4,2,5]{3,2,1,0:T(2,128)S(1)}, f32[16,4,5,2,512]{4,2,3,1,0:T(8,128)S(1)}) fusion(pred[16,512]{1,0:T(8,128)(4,1)S(1)} %iota_compare_fusion, bf16[16,512,4,128,1]{3,2,1,0,4:T(4,128)(2,1)} %bitcast.59, bf16[16,5,4,2,64]{4,1,3,2,0:T(8,128)(2,1)S(1)} %copy.24, bf16[16,5,4,2,64]{4,1,3,2,0:T(8,128)(2,1)S(1)} %copy.23), kind=kOutput, calls=%fused_computation.10 | convolution fusion | flops 85196160 | bytes 9873920 | tf_op jit(solution)/shard_map/rskge,rcke->rkgsc/dot_general | solution.py:43
  75.2 0.3 fusion.26
  75.5 1.0 fusion.6
  76.5 0.0 slice-done.3
  76.5 0.0 slice-done.4
  76.5 2.1 %fusion.14 = f32[16,5,4,2,128]{4,1,3,2,0:T(8,128)S(1)} fusion(bf16[16,512,4,128,1]{3,2,1,0,4:T(4,128)(2,1)S(1)} %bitcast.70, f32[16,4,5,2,512]{4,2,3,1,0:T(8,128)S(1)} %get-tuple-element.24, f32[16,4,2,5]{3,2,1,0:T(2,128)S(1)} %add.50, f32[16,4,2,5]{3,2,1,0:T(2,128)S(1)} %max.7, pred[16,512]{1,0:T(8,128)(4,1)S(1)} %iota_compare_fusion), kind=kOutput, calls=%fused_computation.24 | convolution fusion | flops 85524480 | bytes 10040320 | tf_op jit(solution)/shard_map/rkgsc,rcke->rskge/dot_general | solution.py:62
  78.6 0.0 copy-done.4
  78.6 0.3 fusion.20
  79.0 0.1 copy.31
  79.1 0.1 convert_element_type.56
  79.2 0.0 copy-start.3
  79.2 0.0 slice-start
  79.2 0.0 slice-start.1
  79.2 5.6 %convolution_convert_fusion.1.part = bf16[80,4608]{1,0:T(8,128)(2,1)S(1)} fusion(bf16[80,1024]{1,0:T(8,128)(2,1)S(1)} %convert_element_type.56, bf16[1024,4608]{1,0:T(8,128)(2,1)} %param.22), kind=kOutput, calls=%fused_computation.5 | convolution fusion | flops 755343360 | bytes 10338304 | tf_op jit(solution)/shard_map/dot_general | solution.py:557
  84.8 0.0 copy-done.3
  84.8 36.5 %shard_map.168 = (bf16[320,4608]{1,0:T(8,128)(2,1)S(1)}, bf16[80,1152]{1,0:T(8,128)(2,1)S(1)}) custom-call(bf16[80,4608]{1,0:T(8,128)(2,1)S(1)} %convolution_convert_fusion.1.part, bf16[80,1152]{1,0:T(8,128)(2,1)S(1)} %copy-done.3, f32[1,1152]{1,0:T(1,128)S(1)} %broadcast_in_dim.50.post_ref, f32[1,1152]{1,0:T(1,128)S(1)} %broadcast_in_dim.51.gain_ref), custom_call_target="tpu_custom_call" | custom-call | tf_op jit(solution)/shard_map/pallas_call | solution.py:459
  121.3 0.0 slice-start.2
  121.4 6.9 %fusion.36 = f32[320,1152]{1,0:T(8,128)S(1)} fusion(bf16[320,4608]{1,0:T(8,128)(2,1)S(1)} %get-tuple-element.9, bf16[1152,4608]{1,0:T(8,128)(2,1)} %param.23), kind=kOutput, calls=%fused_computation.64 | convolution fusion | flops 3397386240 | bytes 15040512 | tf_op jit(solution)/shard_map/dot_general | solution.py:586
  128.3 0.0 slice-done
  128.3 0.0 slice-done.1
  128.3 0.0 slice-done.2
  128.3 4.0 %fusion.4 = bf16[320,1152]{1,0:T(8,128)(2,1)S(1)} fusion(bf16[320,4608]{1,0:T(8,128)(2,1)S(1)} %get-tuple-element.9, bf16[1152,4608]{1,0:T(8,128)(2,1)S(1)} %bitcast.67, f32[320,1152]{1,0:T(8,128)S(1)} %fusion.36), kind=kOutput, calls=%fused_computation.7 | convolution fusion | flops 3401072640 | bytes 15777792 | tf_op jit(solution)/shard_map/dot_general | solution.py:587
  132.4 0.0 copy-start.1
  132.4 8.6 %convolution_convert_fusion.part = bf16[320,4608]{1,0:T(8,128)(2,1)S(1)} fusion(bf16[320,1152]{1,0:T(8,128)(2,1)S(1)} %fusion.4, bf16[1152,4608]{1,0:T(8,128)(2,1)} %param.25), kind=kOutput, calls=%fused_computation.4 | convolution fusion | flops 3398860800 | bytes 14303232 | tf_op jit(solution)/shard_map/dot_general | solution.py:589
  141.0 32.0 %shard_map.169 = bf16[80,1152]{1,0:T(8,128)(2,1)S(1)} custom-call(bf16[320,4608]{1,0:T(8,128)(2,1)S(1)} %convolution_convert_fusion.part, bf16[80,1152]{1,0:T(8,128)(2,1)S(1)} %get-tuple-element.10.mid_ref, f32[1,1152]{1,0:T(1,128)S(1)} %broadcast_in_dim.52.post_ref), custom_call_target="tpu_custom_call" | custom-call | tf_op jit(solution)/shard_map/pallas_call | solution.py:459
  173.0 0.7 copy.56
  173.6 0.0 copy-done.1
  (12 shorter events, 0.2 us)
Async XLA Ops:
  0.6 28.0 %copy-start = (bf16[1152,1024]{1,0:T(8,128)(2,1)S(1)}, bf16[1152,1024]{1,0:T(8,128)(2,1)}, u32[]{:S(2)}) copy-start(bf16[1152,1024]{1,0:T(8,128)(2,1)} %param.19) | copy-start | bytes 7077892
  5.4 0.9 copy-start.2
  6.3 21.7 %copy-start.5 = (bf16[1152,512]{1,0:T(8,128)(2,1)S(1)}, bf16[1152,512]{1,0:T(8,128)(2,1)}, u32[]{:S(2)}) copy-start(bf16[1152,512]{1,0:T(8,128)(2,1)} %param.20) | copy-start | bytes 3538948
  66.1 12.5 %copy-start.4 = (bf16[16,5,4,128]{3,2,1,0:T(4,128)(2,1)}, bf16[16,5,4,128]{3,2,1,0:T(4,128)(2,1)S(1)}, u32[]{:S(2)}) copy-start(bf16[16,5,4,128]{3,2,1,0:T(4,128)(2,1)S(1)} %reshape.142) | copy-start | bytes 245764
  67.7 8.8 %slice-start.3 = ((s8[8388608]{0:T(1024)(128)(4,1)}), s8[4194304]{0:T(1024)(128)(4,1)S(1)}, s32[]{:S(2)}) async-start(s8[8388608]{0:T(1024)(128)(4,1)} %bitcast.68), calls=%async_computation.3 | async-start | bytes 8388608
  69.1 7.4 %slice-start.4 = ((s8[8388608]{0:T(1024)(128)(4,1)}), s8[4194304]{0:T(1024)(128)(4,1)S(1)}, s32[]{:S(2)}) async-start(s8[8388608]{0:T(1024)(128)(4,1)} %bitcast.68), calls=%async_computation.4 | async-start | bytes 8388608
  79.2 5.6 %copy-start.3 = (bf16[80,1152]{1,0:T(8,128)(2,1)S(1)}, bf16[80,1152]{1,0:T(8,128)(2,1)}, u32[]{:S(2)}) copy-start(bf16[80,1152]{1,0:T(8,128)(2,1)} %x_ref.3) | copy-start | bytes 552964
  79.2 49.0 %slice-start = ((s8[10616832]{0:T(1024)(128)(4,1)}), s8[4194304]{0:T(1024)(128)(4,1)S(1)}, s32[]{:S(2)}) async-start(s8[10616832]{0:T(1024)(128)(4,1)} %bitcast.66), calls=%async_computation | async-start | bytes 8388608
  79.2 49.0 %slice-start.1 = ((s8[10616832]{0:T(1024)(128)(4,1)}), s8[4194304]{0:T(1024)(128)(4,1)S(1)}, s32[]{:S(2)}) async-start(s8[10616832]{0:T(1024)(128)(4,1)} %bitcast.66), calls=%async_computation.1 | async-start | bytes 8388608
  121.3 6.9 %slice-start.2 = ((s8[10616832]{0:T(1024)(128)(4,1)}), s8[2228224]{0:T(1024)(128)(4,1)S(1)}, s32[]{:S(2)}) async-start(s8[10616832]{0:T(1024)(128)(4,1)} %bitcast.66), calls=%async_computation.2 | async-start | bytes 4456448
  132.4 41.3 %copy-start.1 = (bf16[1152,1024]{1,0:T(8,128)(2,1)S(1)}, bf16[1152,1024]{1,0:T(8,128)(2,1)}, u32[]{:S(2)}) copy-start(bf16[1152,1024]{1,0:T(8,128)(2,1)} %param.19) | copy-start | bytes 7077892

commit v2 on v1

--- a/solution.py
+++ b/solution.py
@@ -1,4 +1,5 @@
 import functools
+import math
 
 import jax
 import jax.numpy as jnp
@@ -31,41 +32,6 @@
 
 def scaling(total):
     return lax.rsqrt(total / D + EPSILON)[:, None]
-
-
-def attend(queries, new_keys, new_values, cache_keys, cache_values, lengths):
-    req_count, steps, heads, size = queries.shape
-    shared = new_keys.shape[2]
-    group = heads // shared
-    scale = (D // HEADS) ** (-0.5)
-    grouped = queries.reshape(req_count, steps, shared, group, size)
-    older = (
-        jnp.einsum("rskge,rcke->rkgsc", grouped, cache_keys, preferred_element_type=jnp.float32)
-        * scale
-    )
-    newer = (
-        jnp.einsum("rskge,rtke->rkgst", grouped, new_keys, preferred_element_type=jnp.float32)
-        * scale
-    )
-    valid = jnp.arange(cache_keys.shape[1], dtype=jnp.int32)[None, :] < lengths[:, None]
-    older = jnp.where(valid[:, None, None, None, :], older, NEGATIVE)
-    causal = (
-        jnp.arange(steps, dtype=jnp.int32)[:, None] >= jnp.arange(steps, dtype=jnp.int32)[None, :]
-    )
-    newer = jnp.where(causal, newer, NEGATIVE)
-    highest = jnp.maximum(jnp.max(older, axis=-1), jnp.max(newer, axis=-1))[..., None]
-    far_mass = jnp.exp(older - highest)
-    near_mass = jnp.exp(newer - highest)
-    total_mass = (jnp.sum(far_mass, axis=-1) + jnp.sum(near_mass, axis=-1))[..., None]
-    far_weights = (far_mass / total_mass).astype(jnp.bfloat16)
-    near_weights = (near_mass / total_mass).astype(jnp.bfloat16)
-    blended = jnp.einsum(
-        "rkgsc,rcke->rskge", far_weights, cache_values, preferred_element_type=jnp.float32
-    )
-    blended = blended + jnp.einsum(
-        "rkgst,rtke->rskge", near_weights, new_values, preferred_element_type=jnp.float32
-    )
-    return blended.reshape(req_count * steps, heads * size).astype(jnp.bfloat16)
 
 
 LANES = 128
@@ -141,7 +107,7 @@
 
 
 def gather_kernel(
-    blks, reqs, x_ref, gain_ref, out, scale_ref, ybuf, sums, ss, sr, s0, zsend, recv, psend, xsend
+    blks, reqs, x_ref, gains, out, scale_ref, ybuf, sums, ss, sr, s0, zsend, recv, psend, xsend
 ):
     b, r = greet(blks, reqs)
     per = blks // reqs
@@ -152,7 +118,7 @@
     home = b // per
     mine = lax.rem(b, per)
     states = x_ref[...].astype(F32)
-    ybuf[...] = (states * gain_ref[...]).astype(BF)
+    ybuf[...] = (states * gains[0:1, :]).astype(BF)
 
     @pl.when(r != home)
     def _():
@@ -237,11 +203,10 @@
     step(r > d, r == reqs - 1, right, rsend, rrecv, r - 1)
 
 
-def chain_order(reqs):
-    order = []
-    for k in range(reqs):
-        order.append(reqs - 1 - k // 2 if k % 2 == 0 else k // 2)
-    return order
+def chain_place(reqs, r, i):
+    low = jnp.where(i < reqs - 1 - r, reqs - 1 - i, i - (reqs - 1 - r))
+    high = jnp.where(i < r, i, reqs - 1 - (i - r))
+    return jnp.where(i == reqs - 1, r, jnp.where(r < reqs // 2, low, high))
 
 
 def chain_end(reqs, r, part, left, right, lsend, lrecv, rsend, rrecv, total):
@@ -272,7 +237,8 @@
     blks, reqs, part, scale_ref, out, left, right, lsend, lrecv, rsend, rrecv
 ):
     b, r = greet(blks, reqs)
-    for d in chain_order(reqs):
+    for i in range(reqs - 1):
+        d = chain_place(reqs, r, i)
         chain_step(reqs, r, d, part, left, right, lsend, lrecv, rsend, rrecv)
     chain_end(reqs, r, part, left, right, lsend, lrecv, rsend, rrecv, out)
     out[...] = out[...] * scale_ref[:, 0:1]
@@ -290,9 +256,9 @@
 
 
 def middle_kernel(
-    blks, reqs, part, x_ref, post_ref, gain_ref, full, mid_ref,
+    blks, reqs, part, x_ref, gains, full, mid_ref, scales,
     rp, rx, own, sums1, sums2, psend0, precv0, xsend0, xrecv0, ss1, sr1, ss2, sr2,
-    s0, zsend, recv, psend, xsend,
+    s0, zsend, recv, psend, xsend, csend, crecv,
 ):
     b, r = greet(blks, reqs)
     chips = blks // 2
@@ -317,12 +283,11 @@
         mixed = mixed + rx[k].astype(F32)
     send_sums(jnp.sum(mixed * mixed, axis=1, keepdims=True), sums1, ss1, sr1, b, blks)
     total = take_sums(rows, sums1, ss1, sr1, b, blks)
-    middle = (x_ref[...].astype(F32) + mixed * inverse(total) * post_ref[...]).astype(BF)
+    middle = (x_ref[...].astype(F32) + mixed * inverse(total) * gains[1:2, :]).astype(BF)
     mid_ref[...] = middle
     wide = middle.astype(F32)
+    own[...] = (wide * gains[2:3, :]).astype(BF)
     send_sums(jnp.sum(wide * wide, axis=1, keepdims=True), sums2, ss2, sr2, b, blks)
-    total = take_sums(rows, sums2, ss2, sr2, b, blks)
-    own[...] = (wide * inverse(total) * gain_ref[...]).astype(BF)
     copy = pltpu.make_async_copy(own, view(full, b, r), s0)
     copy.start()
 
@@ -363,6 +328,12 @@
             call()
 
     spread(r, own, 0)
+    total = take_sums(rows, sums2, ss2, sr2, b, blks)
+    packed = jnp.sum(jnp.where(diagonal(rows), inverse(total), 0.0), axis=0, keepdims=True)
+    scales[r] = jnp.broadcast_to(packed, (8, LANES))
+    for k in range(1, reqs):
+        to = lax.rem(r + k, reqs)
+        remote(scales.at[r], scales.at[r], csend.at[k], crecv.at[k], req=to).start()
     for dist in range(1, reqs):
 
         def up():
@@ -383,6 +354,9 @@
     within(r - reqs + 1, lambda: relay(r - reqs + 1))
     within(r + reqs - 1, lambda: relay(r + reqs - 1))
     copy.wait()
+    for k in range(1, reqs):
+        src = lax.rem(r + reqs - k, reqs)
+        remote(scales.at[src], scales.at[src], csend.at[k], crecv.at[k], req=src).wait()
     for xp in range(chips):
         for d in range(reqs):
             arrive(2 * xp + 1 - c, d)
@@ -408,7 +382,7 @@
 
 
 def last_kernel(
-    blks, reqs, part, mid_ref, post_ref, out,
+    blks, reqs, part, mid_ref, gains, out,
     rp, rx, own, left, right, acc, sums, psend, precv, xsend, xrecv,
     lsend, lrecv, rsend, rrecv, ss, sr,
 ):
@@ -417,7 +391,7 @@
     x, c = b // 2, lax.rem(b, 2)
     mate = b + 1 - 2 * c
     rows = mid_ref.shape[0]
-    order = chain_order(reqs)
+    order = [chain_place(reqs, r, i) for i in range(reqs)]
     for d in order:
         for k in list(range(1, chips)) + [0]:
             xp = lax.rem(x + k, chips)
@@ -451,19 +425,93 @@
             if k:
                 remote(slot, slot, xsend.at[k, d], xrecv.at[k, d], blk=mate).wait_send()
     total = take_sums(rows, sums, ss, sr, b, blks)
-    out[...] = (mid_ref[...].astype(F32) + ffn * inverse(total) * post_ref[...]).astype(BF)
+    out[...] = (mid_ref[...].astype(F32) + ffn * inverse(total) * gains[3:4, :]).astype(BF)
+
+
+def attend_kernel(
+    shared, group, steps, lengths, queries, new_keys, new_values, old_keys, old_values, out
+):
+    heads = shared * group
+    rows = steps * heads
+    scale = (D // HEADS) ** (-0.5)
+    length = lengths[pl.program_id(0)]
+    row = lax.broadcasted_iota(jnp.int32, (rows, 1), 0)
+    mine, step = lax.rem(row, heads) // group, row // heads
+
+    def scores(keys):
+        value = lax.dot_general(
+            queries[0], keys, (((1,), (1,)), ((), ())), preferred_element_type=F32
+        )
+        col = lax.broadcasted_iota(jnp.int32, (1, keys.shape[0]), 1)
+        return value * scale, lax.rem(col, shared), col // shared
+
+    older, owner, slot = scores(old_keys[0])
+    owner = jnp.where(slot < length, owner, -1)
+    older = jnp.where(owner == mine, older, NEGATIVE)
+    newer, owner, slot = scores(new_keys[0])
+    newer = jnp.where(jnp.logical_and(owner == mine, slot <= step), newer, NEGATIVE)
+    highest = jnp.maximum(
+        jnp.max(older, axis=1, keepdims=True), jnp.max(newer, axis=1, keepdims=True)
+    )
+    far, near = jnp.exp(older - highest), jnp.exp(newer - highest)
+    mass = 1.0 / (jnp.sum(far, axis=1, keepdims=True) + jnp.sum(near, axis=1, keepdims=True))
+    blended = jnp.dot((far * mass).astype(BF), old_values[0], preferred_element_type=F32)
+    blended += jnp.dot((near * mass).astype(BF), new_values[0], preferred_element_type=F32)
+    out[0] = blended.astype(BF)
+
+
+def attend(queries, new_keys, new_values, cache_keys, cache_values, lengths):
+    count, slots, shared, size = cache_keys.shape
+    steps = queries.shape[0] // count
+    group = queries.shape[1] // shared
+    rows = steps * shared * group
+
+    def block(height):
+        return pl.BlockSpec((1, height, size), lambda i: (i, 0, 0))
+
+    out = pl.pallas_call(
+        functools.partial(attend_kernel, shared, group, steps),
+        grid=(count,),
+        out_shape=jax.ShapeDtypeStruct((count, rows, size), BF),
+        in_specs=[
+            pl.BlockSpec(memory_space=pltpu.SMEM),
+            block(rows),
+            block(steps * shared),
+            block(steps * shared),
+            block(slots * shared),
+            block(slots * shared),
+        ],
+        out_specs=block(rows),
+        compiler_params=pltpu.CompilerParams(vmem_limit_bytes=57 * 2**20),
+    )(
+        lengths,
+        queries.reshape(count, rows, size),
+        new_keys.reshape(count, steps * shared, size),
+        new_values.reshape(count, steps * shared, size),
+        cache_keys.reshape(count, slots * shared, size),
+        cache_values.reshape(count, slots * shared, size),
+    )
+    return out.reshape(count * steps, shared * group * size)
 
 
 def call(kernel, sizes, number, outs, scratch, *args):
     vmem = pl.BlockSpec(memory_space=pltpu.VMEM)
+    held = 0
+    for leaf in list(args) + jax.tree.leaves(outs) + scratch:
+        if hasattr(leaf.dtype, "itemsize"):
+            *lead, second, last = leaf.shape
+            padded = math.prod(lead) * (second + 15) * (last + LANES - 1)
+            held += padded * leaf.dtype.itemsize
+    limit = min(held + 6 * 2**20, 60 * 2**20)
     return pl.pallas_call(
         functools.partial(kernel, *sizes),
         out_shape=outs,
         in_specs=[vmem] * len(args),
         out_specs=jax.tree.map(lambda _: vmem, outs),
         scratch_shapes=scratch,
+        cost_estimate=pl.CostEstimate(flops=10**10, bytes_accessed=10**8, transcendentals=0),
         compiler_params=pltpu.CompilerParams(
-            collective_id=number, has_side_effects=True, vmem_limit_bytes=40 * 2**20
+            collective_id=number, has_side_effects=True, vmem_limit_bytes=limit
         ),
     )(*args)
 
@@ -499,6 +547,7 @@
     heads_local = query_cols // size
     shape = jax.ShapeDtypeStruct
     sums = pltpu.VMEM((blks, 8, LANES), F32)
+    gains = jnp.stack([attn_gain, post_attn_gain, ffn_gain, post_ffn_gain])
     gathered, scale = call(
         gather_kernel,
         sizes,
@@ -516,7 +565,7 @@
             DMA((chips, reqs)),
         ],
         hidden_states,
-        attn_gain[None, :],
+        gains,
     )
     slices = gathered.transpose(1, 2, 0, 3).reshape(reqs * rows, per * width)
     parts = jnp.concatenate(
@@ -547,24 +596,20 @@
     draft_keys = new_keys.reshape(req_count, steps, kv_local, size)
     draft_values = value_lin.astype(BF).reshape(req_count, steps, kv_local, size)
     attended = attend(
-        queries.reshape(req_count, steps, heads_local, size),
-        draft_keys,
-        draft_values,
-        cache_keys,
-        cache_values,
-        context_lengths,
+        queries, draft_keys, draft_values, cache_keys, cache_values, context_lengths
     )
     mixed = jnp.dot(attended, o_weight, preferred_element_type=F32).astype(BF)
     flat = width % LANES == 0 and rows % 16 == 0
     if not flat:
         mixed = mixed.reshape(rows, blks, width).transpose(1, 0, 2)
-    full, middle = call(
+    full, middle, scales = call(
         middle_kernel,
         sizes,
         2,
         (
             shape((reqs * rows, D) if flat else (blks, reqs, rows, width), BF),
             shape((rows, width), BF),
+            shape((reqs, 8, LANES), F32),
         ),
         [
             pltpu.VMEM((chips, rows, width), BF),
@@ -575,16 +620,18 @@
         ]
         + [DMA((chips,))] * 4
         + [DMA((blks,))] * 4
-        + [DMA, DMA((2, reqs)), DMA((blks, reqs)), DMA((chips, reqs)), DMA((chips, reqs))],
+        + [DMA, DMA((2, reqs)), DMA((blks, reqs)), DMA((chips, reqs)), DMA((chips, reqs))]
+        + [DMA((reqs,))] * 2,
         mixed,
         hidden_states,
-        post_attn_gain[None, :],
-        ffn_gain[None, :],
+        gains,
     )
     if not flat:
         full = full.transpose(1, 2, 0, 3).reshape(reqs * rows, D)
     gate = lax.dot_general(full, gate_weight, (((1,), (1,)), ((), ())), preferred_element_type=F32)
     up = lax.dot_general(full, up_weight, (((1,), (1,)), ((), ())), preferred_element_type=F32)
+    scales = scales[:, 0, :rows].reshape(reqs * rows, 1)
+    gate, up = gate * scales, up * scales
     hidden = (jax.nn.gelu(gate, approximate=True) * up).astype(BF)
     terms = jnp.dot(hidden, down_weight, preferred_element_type=F32).astype(BF)
     if not flat:
@@ -602,7 +649,7 @@
         + [DMA((blks,))] * 2,
         terms,
         middle,
-        post_ffn_gain[None, :],
+        gains,
     )
     return (layer_output, draft_keys, draft_values)
 

time: 176 us -> 171 us (0.972); the launches traced: 174 us -> 171 us
  matrix products: 38.4 us -> 28.3 us
  local copies, waits for them, and re-layouts: 5.96 us -> 9.63 us
  Pallas kernels: 125 us -> 128 us
    pallas_call x0 -> x1, Pallas kernels: none -> 17.8 us  [attend(): pl.pallas_call(functools.partial(attend_kernel, shared, group, steps), gr...]
    pallas_call x4, Pallas kernels: 125 us -> 110 us  [call(): pl.pallas_call(functools.partial(kernel, *sizes), out_shape=outs, in_spec...]
    dot_general x4 -> x0, matrix products: 9.81 us -> none  [the longest x1 6.02 us: attend(): jnp.einsum('rskge,rcke->rkgsc', grouped, cache_keys, preferred_element_ty...]
    dot_general x1, matrix products: 8.62 us -> 4.24 us  [body(): terms = jnp.dot(hidden, down_weight, preferred_element_type=F32).astype(BF)]
    another operation x0 -> x5, local copies, waits for them, and re-layouts: none -> 3.68 us  [the longest x4 2.95 us: body(): gains = jnp.stack([attn_gain, post_attn_gain, ffn_gain, post_ffn_gain])]
    dot_general x1, matrix products: 4.05 us -> 7.17 us  [body(): lax.dot_general(full, up_weight, (((1,), (1,)), ((), ())), preferred_elem...]
    broadcast_in_dim x4 -> x0, local copies, waits for them, and re-layouts: 2.95 us -> none  [the longest x1 0.85 us: body(): attn_gain[None, :]]
    dot_general x1, matrix products: 6.89 us -> 9.19 us  [body(): lax.dot_general(full, gate_weight, (((1,), (1,)), ((), ())), preferred_el...]
where the time goes in v2:
time: 171 us
  Pallas kernels  128 us (75%)
  matrix products  28.3 us (17%)
  local copies, waits for them, and re-layouts  9.63 us (6%)
  other arithmetic  3.8 us (2%)
    pallas_call x4, Pallas kernels, call(): pl.pallas_call(functools.partial(kernel, *sizes), out_shape=outs, in_spec...  110 us
    pallas_call x1, Pallas kernels, attend(): pl.pallas_call(functools.partial(attend_kernel, shared, group, steps), gr...  17.8 us
    dot_general x1, matrix products, body(): lax.dot_general(full, gate_weight, (((1,), (1,)), ((), ())), preferred_el...  9.19 us
    dot_general x1, matrix products, body(): lax.dot_general(full, up_weight, (((1,), (1,)), ((), ())), preferred_elem...  7.17 us
    dot_general x1, matrix products, body(): mixed = jnp.dot(attended, o_weight, preferred_element_type=F32).astype(BF)  5.47 us
    dot_general x1, matrix products, body(): terms = jnp.dot(hidden, down_weight, preferred_element_type=F32).astype(BF)  4.24 us
    unnamed x25, local copies, waits for them, and re-layouts  3.96 us

profile of v2, /device:TPU:0, one launch (start us, length us, event | category | flops | bytes accessed | tf_op | source)
XLA Modules:
  0.0 170.6 jit_solution(302850070947455627)
XLA Ops:
  0.6 0.0 copy-start
  0.7 0.9 stack.15
  1.5 0.7 stack.16
  2.2 0.7 stack.17
  2.9 0.7 stack.18
  3.6 0.7 add_convert_fusion.2
  4.4 0.1 convert_element_type.41
  4.5 0.2 multiply_cosine_fusion
  4.7 0.0 copy-start.2
  4.7 0.9 copy-done.2
  5.6 0.0 copy-start.6
  5.6 19.8 %shard_map.166 = (bf16[1,4,80,1152]{3,2,1,0:T(8,128)(2,1)S(1)}, f32[80,128]{1,0:T(8,128)S(1)}) custom-call(bf16[80,1152]{1,0:T(8,128)(2,1)S(1)} %copy-done.2, f32[4,1152]{1,0:T(4,128)S(1)} %pad_maximum_fusion.4.gains), custom_call_target="tpu_custom_call" | custom-call | flops 10000000000 | bytes 100000000 | tf_op jit(solution)/shard_map/pallas_call | solution.py:506
  25.5 0.0 copy-start.7
  25.5 0.0 copy-done.6
  25.5 0.6 convolution_convert_fusion.3
  26.1 0.7 copy-done.7
  26.7 0.6 convolution_convert_fusion.4
  27.3 0.0 copy-done
  27.3 1.1 convolution_convert_fusion.2
  28.4 0.1 pad_maximum_fusion
  28.5 29.0 %shard_map.167 = f32[80,2048]{1,0:T(8,128)S(1)} custom-call(bf16[4,80,2048]{2,1,0:T(8,128)(2,1)S(1)} %bitcast.25, f32[80,128]{1,0:T(8,128)S(1)} %get-tuple-element.9.scale_ref), custom_call_target="tpu_custom_call" | custom-call | flops 10000000000 | bytes 100000000 | tf_op jit(solution)/shard_map/pallas_call | solution.py:506
  57.6 0.7 reshape.132
  58.2 0.7 reshape_reshape.4.new_values
  59.0 0.1 copy.18
  59.1 0.1 reshape.128
  59.1 0.2 subtract_convert_fusion.1
  59.3 0.2 subtract_convert_fusion
  59.5 0.8 pad_maximum_fusion.1.queries
  60.3 0.8 pad_maximum_fusion.3
  61.2 0.7 pad_maximum_fusion.2.new_keys
  61.9 17.8 %shard_map.168 = bf16[16,40,128]{2,1,0:T(8,128)(2,1)} custom-call(s32[16]{0:T(128)} %lengths.1, bf16[16,40,128]{2,1,0:T(8,128)(2,1)} %pad_maximum_fusion.1.queries, bf16[16,20,128]{2,1,0:T(8,128)(2,1)} %pad_maximum_fusion.2.new_keys, bf16[16,20,128]{2,1,0:T(8,128)(2,1)} %reshape_reshape.4.new_values, bf16[16,2048,128]{2,1,0:T(8,128)(2,1)} %bitcast.29, ...), custom_call_target="tpu_custom_call" | custom-call | tf_op jit(solution)/shard_map/pallas_call | solution.py:472
  79.7 1.0 reshape.131
  80.7 0.0 copy-start.3
  80.7 5.5 %convolution_convert_fusion.1.part = bf16[80,4608]{1,0:T(8,128)(2,1)S(1)} fusion(bf16[80,1024]{1,0:T(8,128)(2,1)S(1)} %reshape.131, bf16[1024,4608]{1,0:T(8,128)(2,1)} %param.22), kind=kOutput, calls=%fused_computation.1 | convolution fusion | flops 755343360 | bytes 10338304 | tf_op jit(solution)/shard_map/dot_general | solution.py:601
  86.2 0.0 copy-done.3
  86.2 33.6 %shard_map.169 = (bf16[320,4608]{1,0:T(8,128)(2,1)S(1)}, bf16[80,1152]{1,0:T(8,128)(2,1)S(1)}, f32[4,8,128]{2,1,0:T(8,128)S(1)}) custom-call(bf16[80,4608]{1,0:T(8,128)(2,1)S(1)} %convolution_convert_fusion.1.part, bf16[80,1152]{1,0:T(8,128)(2,1)S(1)} %copy-done.3, f32[4,1152]{1,0:T(4,128)S(1)} %pad_maximum_fusion.4.gains), custom_call_target="tpu_custom_call" | custom-call | flops 10000000000 | bytes 100000000 | tf_op jit(solution)/shard_map/pallas_call | solution.py:506
  119.8 0.0 copy-start.4
  119.8 1.6 copy-done.4
  121.4 0.1 mul.148
  121.5 0.0 copy-start.5
  121.5 0.0 slice-start
  121.5 0.0 slice-start.1
  121.5 9.2 %fusion.8 = f32[320,1152]{1,0:T(8,128)S(1)} fusion(bf16[320,4608]{1,0:T(8,128)(2,1)} %copy-done.4, bf16[1152,4608]{1,0:T(8,128)(2,1)} %param.23, f32[320]{0:T(512)S(1)} %mul.148), kind=kOutput, calls=%fused_computation.13 | convolution fusion | flops 3400704000 | bytes 15041792 | tf_op jit(solution)/shard_map/dot_general | solution.py:631
  130.7 0.0 copy-done.5
  130.7 0.0 slice-start.2
  130.7 7.2 %fusion.1 = bf16[320,1152]{1,0:T(8,128)(2,1)S(1)} fusion(f32[320,1152]{1,0:T(8,128)S(1)} %fusion.8, bf16[320,4608]{1,0:T(8,128)(2,1)S(1)} %copy-done.5, bf16[1152,4608]{1,0:T(8,128)(2,1)} %param.24, f32[320]{0:T(512)S(1)} %mul.148), kind=kOutput, calls=%fused_computation.5 | convolution fusion | flops 3398492160 | bytes 15779072 | tf_op jit(solution)/shard_map/dot_general | solution.py:632
  137.9 0.0 slice-done
  137.9 0.0 slice-done.1
  137.9 0.0 slice-done.2
  137.9 4.2 %convolution_convert_fusion.part = bf16[320,4608]{1,0:T(8,128)(2,1)S(1)} fusion(bf16[320,1152]{1,0:T(8,128)(2,1)S(1)} %fusion.1, bf16[1152,4608]{1,0:T(8,128)(2,1)S(1)} %bitcast.37), kind=kOutput, calls=%fused_computation | convolution fusion | flops 3398860800 | bytes 14303232 | tf_op jit(solution)/shard_map/dot_general | solution.py:636
  142.2 0.0 copy-start.1
  142.2 27.7 %shard_map.170 = bf16[80,1152]{1,0:T(8,128)(2,1)S(1)} custom-call(bf16[320,4608]{1,0:T(8,128)(2,1)S(1)} %convolution_convert_fusion.part, bf16[80,1152]{1,0:T(8,128)(2,1)S(1)} %get-tuple-element.12.mid_ref, f32[4,1152]{1,0:T(4,128)S(1)} %pad_maximum_fusion.4.gains), custom_call_target="tpu_custom_call" | custom-call | flops 10000000000 | bytes 100000000 | tf_op jit(solution)/shard_map/pallas_call | solution.py:506
  169.9 0.7 copy.20
  170.6 0.0 copy-done.1
  (9 shorter events, 0.2 us)
Async XLA Ops:
  0.6 26.7 %copy-start = (bf16[1152,1024]{1,0:T(8,128)(2,1)S(1)}, bf16[1152,1024]{1,0:T(8,128)(2,1)}, u32[]{:S(2)}) copy-start(bf16[1152,1024]{1,0:T(8,128)(2,1)} %param.19) | copy-start | bytes 7077892
  4.7 0.9 copy-start.2
  5.6 19.8 %copy-start.6 = (bf16[1152,512]{1,0:T(8,128)(2,1)S(1)}, bf16[1152,512]{1,0:T(8,128)(2,1)}, u32[]{:S(2)}) copy-start(bf16[1152,512]{1,0:T(8,128)(2,1)} %param.21) | copy-start | bytes 3538948
  25.5 1.3 copy-start.7
  80.7 5.5 %copy-start.3 = (bf16[80,1152]{1,0:T(8,128)(2,1)S(1)}, bf16[80,1152]{1,0:T(8,128)(2,1)}, u32[]{:S(2)}) copy-start(bf16[80,1152]{1,0:T(8,128)(2,1)} %x_ref.3) | copy-start | bytes 552964
  119.8 1.6 copy-start.4
  121.5 9.2 %copy-start.5 = (bf16[320,4608]{1,0:T(8,128)(2,1)S(1)}, bf16[320,4608]{1,0:T(8,128)(2,1)}, u32[]{:S(2)}) copy-start(bf16[320,4608]{1,0:T(8,128)(2,1)} %copy-done.4) | copy-start | bytes 8847364
  121.5 16.4 %slice-start = ((s8[10616832]{0:T(1024)(128)(4,1)}), s8[4194304]{0:T(1024)(128)(4,1)S(1)}, s32[]{:S(2)}) async-start(s8[10616832]{0:T(1024)(128)(4,1)} %bitcast.36), calls=%async_computation | async-start | bytes 8388608
  121.5 16.4 %slice-start.1 = ((s8[10616832]{0:T(1024)(128)(4,1)}), s8[4194304]{0:T(1024)(128)(4,1)S(1)}, s32[]{:S(2)}) async-start(s8[10616832]{0:T(1024)(128)(4,1)} %bitcast.36), calls=%async_computation.1 | async-start | bytes 8388608
  130.7 7.2 %slice-start.2 = ((s8[10616832]{0:T(1024)(128)(4,1)}), s8[2228224]{0:T(1024)(128)(4,1)S(1)}, s32[]{:S(2)}) async-start(s8[10616832]{0:T(1024)(128)(4,1)} %bitcast.36), calls=%async_computation.2 | async-start | bytes 4456448
  142.2 28.4 %copy-start.1 = (bf16[1152,1024]{1,0:T(8,128)(2,1)S(1)}, bf16[1152,1024]{1,0:T(8,128)(2,1)}, u32[]{:S(2)}) copy-start(bf16[1152,1024]{1,0:T(8,128)(2,1)} %param.19) | copy-start | bytes 7077892

commit v3 on v2

--- a/solution.py
+++ b/solution.py
@@ -107,7 +107,7 @@
 
 
 def gather_kernel(
-    blks, reqs, x_ref, gains, out, scale_ref, ybuf, sums, ss, sr, s0, zsend, recv, psend, xsend
+    blks, reqs, x_ref, gain_ref, out, scale_ref, ybuf, sums, ss, sr, s0, zsend, recv, psend, xsend
 ):
     b, r = greet(blks, reqs)
     per = blks // reqs
@@ -118,7 +118,7 @@
     home = b // per
     mine = lax.rem(b, per)
     states = x_ref[...].astype(F32)
-    ybuf[...] = (states * gains[0:1, :]).astype(BF)
+    ybuf[...] = (states * gain_ref[...][None, :]).astype(BF)
 
     @pl.when(r != home)
     def _():
@@ -256,7 +256,7 @@
 
 
 def middle_kernel(
-    blks, reqs, part, x_ref, gains, full, mid_ref, scales,
+    blks, reqs, part, x_ref, post_ref, gain_ref, full, mid_ref, scales,
     rp, rx, own, sums1, sums2, psend0, precv0, xsend0, xrecv0, ss1, sr1, ss2, sr2,
     s0, zsend, recv, psend, xsend, csend, crecv,
 ):
@@ -283,10 +283,10 @@
         mixed = mixed + rx[k].astype(F32)
     send_sums(jnp.sum(mixed * mixed, axis=1, keepdims=True), sums1, ss1, sr1, b, blks)
     total = take_sums(rows, sums1, ss1, sr1, b, blks)
-    middle = (x_ref[...].astype(F32) + mixed * inverse(total) * gains[1:2, :]).astype(BF)
+    middle = (x_ref[...].astype(F32) + mixed * inverse(total) * post_ref[...][None, :]).astype(BF)
     mid_ref[...] = middle
     wide = middle.astype(F32)
-    own[...] = (wide * gains[2:3, :]).astype(BF)
+    own[...] = (wide * gain_ref[...][None, :]).astype(BF)
     send_sums(jnp.sum(wide * wide, axis=1, keepdims=True), sums2, ss2, sr2, b, blks)
     copy = pltpu.make_async_copy(own, view(full, b, r), s0)
     copy.start()
@@ -382,7 +382,7 @@
 
 
 def last_kernel(
-    blks, reqs, part, mid_ref, gains, out,
+    blks, reqs, part, mid_ref, post_ref, out,
     rp, rx, own, left, right, acc, sums, psend, precv, xsend, xrecv,
     lsend, lrecv, rsend, rrecv, ss, sr,
 ):
@@ -425,73 +425,42 @@
             if k:
                 remote(slot, slot, xsend.at[k, d], xrecv.at[k, d], blk=mate).wait_send()
     total = take_sums(rows, sums, ss, sr, b, blks)
-    out[...] = (mid_ref[...].astype(F32) + ffn * inverse(total) * gains[3:4, :]).astype(BF)
-
-
-def attend_kernel(
-    shared, group, steps, lengths, queries, new_keys, new_values, old_keys, old_values, out
-):
-    heads = shared * group
-    rows = steps * heads
+    out[...] = (mid_ref[...].astype(F32) + ffn * inverse(total) * post_ref[...][None, :]).astype(BF)
+
+
+def attend(queries, new_keys, new_values, cache_keys, cache_values, lengths):
+    req_count, steps, heads, size = queries.shape
+    shared = new_keys.shape[2]
+    group = heads // shared
     scale = (D // HEADS) ** (-0.5)
-    length = lengths[pl.program_id(0)]
-    row = lax.broadcasted_iota(jnp.int32, (rows, 1), 0)
-    mine, step = lax.rem(row, heads) // group, row // heads
-
-    def scores(keys):
-        value = lax.dot_general(
-            queries[0], keys, (((1,), (1,)), ((), ())), preferred_element_type=F32
-        )
-        col = lax.broadcasted_iota(jnp.int32, (1, keys.shape[0]), 1)
-        return value * scale, lax.rem(col, shared), col // shared
-
-    older, owner, slot = scores(old_keys[0])
-    owner = jnp.where(slot < length, owner, -1)
-    older = jnp.where(owner == mine, older, NEGATIVE)
-    newer, owner, slot = scores(new_keys[0])
-    newer = jnp.where(jnp.logical_and(owner == mine, slot <= step), newer, NEGATIVE)
-    highest = jnp.maximum(
-        jnp.max(older, axis=1, keepdims=True), jnp.max(newer, axis=1, keepdims=True)
-    )
-    far, near = jnp.exp(older - highest), jnp.exp(newer - highest)
-    mass = 1.0 / (jnp.sum(far, axis=1, keepdims=True) + jnp.sum(near, axis=1, keepdims=True))
-    blended = jnp.dot((far * mass).astype(BF), old_values[0], preferred_element_type=F32)
-    blended += jnp.dot((near * mass).astype(BF), new_values[0], preferred_element_type=F32)
-    out[0] = blended.astype(BF)
-
-
-def attend(queries, new_keys, new_values, cache_keys, cache_values, lengths):
-    count, slots, shared, size = cache_keys.shape
-    steps = queries.shape[0] // count
-    group = queries.shape[1] // shared
-    rows = steps * shared * group
-
-    def block(height):
-        return pl.BlockSpec((1, height, size), lambda i: (i, 0, 0))
-
-    out = pl.pallas_call(
-        functools.partial(attend_kernel, shared, group, steps),
-        grid=(count,),
-        out_shape=jax.ShapeDtypeStruct((count, rows, size), BF),
-        in_specs=[
-            pl.BlockSpec(memory_space=pltpu.SMEM),
-            block(rows),
-            block(steps * shared),
-            block(steps * shared),
-            block(slots * shared),
-            block(slots * shared),
-        ],
-        out_specs=block(rows),
-        compiler_params=pltpu.CompilerParams(vmem_limit_bytes=57 * 2**20),
-    )(
-        lengths,
-        queries.reshape(count, rows, size),
-        new_keys.reshape(count, steps * shared, size),
-        new_values.reshape(count, steps * shared, size),
-        cache_keys.reshape(count, slots * shared, size),
-        cache_values.reshape(count, slots * shared, size),
-    )
-    return out.reshape(count * steps, shared * group * size)
+    grouped = queries.reshape(req_count, steps, shared, group, size)
+    older = (
+        jnp.einsum("rskge,rcke->rkgsc", grouped, cache_keys, preferred_element_type=jnp.float32)
+        * scale
+    )
+    newer = (
+        jnp.einsum("rskge,rtke->rkgst", grouped, new_keys, preferred_element_type=jnp.float32)
+        * scale
+    )
+    valid = jnp.arange(cache_keys.shape[1], dtype=jnp.int32)[None, :] < lengths[:, None]
+    older = jnp.where(valid[:, None, None, None, :], older, NEGATIVE)
+    causal = (
+        jnp.arange(steps, dtype=jnp.int32)[:, None] >= jnp.arange(steps, dtype=jnp.int32)[None, :]
+    )
+    newer = jnp.where(causal, newer, NEGATIVE)
+    highest = jnp.maximum(jnp.max(older, axis=-1), jnp.max(newer, axis=-1))[..., None]
+    far_mass = jnp.exp(older - highest)
+    near_mass = jnp.exp(newer - highest)
+    total_mass = (jnp.sum(far_mass, axis=-1) + jnp.sum(near_mass, axis=-1))[..., None]
+    far_weights = (far_mass / total_mass).astype(jnp.bfloat16)
+    near_weights = (near_mass / total_mass).astype(jnp.bfloat16)
+    blended = jnp.einsum(
+        "rkgsc,rcke->rskge", far_weights, cache_values, preferred_element_type=jnp.float32
+    )
+    blended = blended + jnp.einsum(
+        "rkgst,rtke->rskge", near_weights, new_values, preferred_element_type=jnp.float32
+    )
+    return blended.reshape(req_count * steps, heads * size).astype(jnp.bfloat16)
 
 
 def call(kernel, sizes, number, outs, scratch, *args):
@@ -499,7 +468,7 @@
     held = 0
     for leaf in list(args) + jax.tree.leaves(outs) + scratch:
         if hasattr(leaf.dtype, "itemsize"):
-            *lead, second, last = leaf.shape
+            *lead, second, last = (1,) + leaf.shape
             padded = math.prod(lead) * (second + 15) * (last + LANES - 1)
             held += padded * leaf.dtype.itemsize
     limit = min(held + 6 * 2**20, 60 * 2**20)
@@ -547,7 +516,6 @@
     heads_local = query_cols // size
     shape = jax.ShapeDtypeStruct
     sums = pltpu.VMEM((blks, 8, LANES), F32)
-    gains = jnp.stack([attn_gain, post_attn_gain, ffn_gain, post_ffn_gain])
     gathered, scale = call(
         gather_kernel,
         sizes,
@@ -565,7 +533,7 @@
             DMA((chips, reqs)),
         ],
         hidden_states,
-        gains,
+        attn_gain,
     )
     slices = gathered.transpose(1, 2, 0, 3).reshape(reqs * rows, per * width)
     parts = jnp.concatenate(
@@ -596,7 +564,7 @@
     draft_keys = new_keys.reshape(req_count, steps, kv_local, size)
     draft_values = value_lin.astype(BF).reshape(req_count, steps, kv_local, size)
     attended = attend(
-        queries, draft_keys, draft_values, cache_keys, cache_values, context_lengths
+        queries.reshape(req_count, steps, heads_local, size), draft_keys, draft_values, cache_keys, cache_values, context_lengths
     )
     mixed = jnp.dot(attended, o_weight, preferred_element_type=F32).astype(BF)
     flat = width % LANES == 0 and rows % 16 == 0
@@ -624,7 +592,8 @@
         + [DMA((reqs,))] * 2,
         mixed,
         hidden_states,
-        gains,
+        post_attn_gain,
+        ffn_gain,
     )
     if not flat:
         full = full.transpose(1, 2, 0, 3).reshape(reqs * rows, D)
@@ -649,7 +618,7 @@
         + [DMA((blks,))] * 2,
         terms,
         middle,
-        gains,
+        post_ffn_gain,
     )
     return (layer_output, draft_keys, draft_values)
 

time: 171 us -> 157 us (0.918)
  Pallas kernels: 128 us -> 110 us
  matrix products: 28.3 us -> 37.1 us
  local copies, waits for them, and re-layouts: 9.63 us -> 4.49 us
    pallas_call x1 -> x0, Pallas kernels: 17.8 us -> none  [attend(): pl.pallas_call(functools.partial(attend_kernel, shared, group, steps), gr...]
    dot_general x0 -> x4, matrix products: none -> 9.71 us  [the longest x1 6.02 us: attend(): jnp.einsum('rskge,rcke->rkgsc', grouped, cache_keys, preferred_element_ty...]
    another operation x5 -> x0, local copies, waits for them, and re-layouts: 3.68 us -> none  [the longest x4 2.95 us: body(): gains = jnp.stack([attn_gain, post_attn_gain, ffn_gain, post_ffn_gain])]
    concatenate x3 -> x1, other arithmetic: 2.27 us -> 0.11 us  [rotate(): jnp.concatenate([first * cosine - second * sine, second * cosine + first...]
    unnamed x25 -> x36, local copies, waits for them, and re-layouts: 3.96 us -> 3.79 us
where the time goes in v3:
time: 157 us
  Pallas kernels  110 us (70%)
  matrix products  37.1 us (24%)
  local copies, waits for them, and re-layouts  4.49 us (3%)
  other arithmetic  3.78 us (2%)
    pallas_call x4, Pallas kernels, call(): pl.pallas_call(functools.partial(kernel, *sizes), out_shape=outs, in_spec...  110 us
    dot_general x1, matrix products, body(): lax.dot_general(full, gate_weight, (((1,), (1,)), ((), ())), preferred_el...  8.3 us
    dot_general x1, matrix products, body(): lax.dot_general(full, up_weight, (((1,), (1,)), ((), ())), preferred_elem...  7.15 us
    dot_general x1, matrix products, attend(): jnp.einsum('rskge,rcke->rkgsc', grouped, cache_keys, preferred_element_ty...  6.02 us
    dot_general x1, matrix products, body(): mixed = jnp.dot(attended, o_weight, preferred_element_type=F32).astype(BF)  5.48 us
    dot_general x1, matrix products, body(): terms = jnp.dot(hidden, down_weight, preferred_element_type=F32).astype(BF)  4.24 us
    unnamed x36, local copies, waits for them, and re-layouts  3.79 us

profile of v3, /device:TPU:0, one launch (start us, length us, event | category | flops | bytes accessed | tf_op | source)
XLA Modules:
  0.0 156.6 jit_solution(980527299314711381)
XLA Ops:
  0.6 0.0 copy-start
  0.7 0.9 iota_compare_fusion
  1.6 0.7 add_convert_fusion.2
  2.3 0.1 convert_element_type.52
  2.4 0.2 multiply_cosine_fusion
  2.6 0.0 copy-start.2
  2.6 0.9 copy-done.2
  3.5 0.0 copy-start.4
  3.5 0.7 copy-done.4
  4.2 0.0 copy-start.9
  4.2 19.8 %shard_map.166 = (bf16[1,4,80,1152]{3,2,1,0:T(8,128)(2,1)S(1)}, f32[80,128]{1,0:T(8,128)S(1)}) custom-call(bf16[80,1152]{1,0:T(8,128)(2,1)S(1)} %copy-done.2, f32[1152]{0:T(1024)S(1)} %copy-done.4), custom_call_target="tpu_custom_call" | custom-call | flops 10000000000 | bytes 100000000 | tf_op jit(solution)/shard_map/pallas_call | solution.py:475
  24.1 0.0 copy-start.10
  24.1 0.0 copy-done.9
  24.1 0.6 convolution_convert_fusion.3
  24.7 0.7 copy-done.10
  25.3 0.6 convolution_convert_fusion.4
  25.9 0.0 copy-done
  25.9 1.0 convolution_convert_fusion.2
  27.0 0.1 pad_maximum_fusion
  27.1 29.0 %shard_map.167 = f32[80,2048]{1,0:T(8,128)S(1)} custom-call(bf16[4,80,2048]{2,1,0:T(8,128)(2,1)S(1)} %bitcast.55, f32[80,128]{1,0:T(8,128)S(1)} %get-tuple-element.9.scale_ref), custom_call_target="tpu_custom_call" | custom-call | flops 10000000000 | bytes 100000000 | tf_op jit(solution)/shard_map/pallas_call | solution.py:475
  56.1 0.0 copy-start.8
  56.2 0.1 copy.44
  56.3 0.1 reshape.142
  56.3 0.2 subtract_convert_fusion.1
  56.5 0.2 subtract_convert_fusion
  56.8 0.1 pad_maximum_fusion.2
  56.9 0.7 copy.32
  57.6 0.1 copy.24
  57.7 0.1 copy.23
  57.7 0.0 slice-start.3
  57.7 1.4 fusion.36
  59.1 0.0 slice-start.4
  59.1 6.0 %bitcast_reduce_fusion = (f32[16,4,2,5]{3,2,1,0:T(2,128)S(1)}, f32[16,4,5,2,512]{4,2,3,1,0:T(8,128)S(1)}) fusion(pred[16,512]{1,0:T(8,128)(4,1)S(1)} %iota_compare_fusion, bf16[16,512,4,128,1]{3,2,1,0,4:T(4,128)(2,1)} %bitcast.59, bf16[16,5,4,2,64]{4,1,3,2,0:T(8,128)(2,1)S(1)} %copy.24, bf16[16,5,4,2,64]{4,1,3,2,0:T(8,128)(2,1)S(1)} %copy.23), kind=kOutput, calls=%fused_computation.12 | convolution fusion | flops 85196160 | bytes 9873920 | tf_op jit(solution)/shard_map/rskge,rcke->rkgsc/dot_general | solution.py:438
  65.2 0.3 fusion.27
  65.5 1.0 fusion.7
  66.5 0.0 slice-done.3
  66.5 0.0 slice-done.4
  66.5 2.0 %fusion.15 = f32[16,5,4,2,128]{4,1,3,2,0:T(8,128)S(1)} fusion(bf16[16,512,4,128,1]{3,2,1,0,4:T(4,128)(2,1)S(1)} %bitcast.70, f32[16,4,5,2,512]{4,2,3,1,0:T(8,128)S(1)} %get-tuple-element.26, f32[16,4,2,5]{3,2,1,0:T(2,128)S(1)} %add.50, f32[16,4,2,5]{3,2,1,0:T(2,128)S(1)} %max.7, pred[16,512]{1,0:T(8,128)(4,1)S(1)} %iota_compare_fusion), kind=kOutput, calls=%fused_computation.26 | convolution fusion | flops 85524480 | bytes 10040320 | tf_op jit(solution)/shard_map/rkgsc,rcke->rskge/dot_general | solution.py:457
  68.5 0.0 copy-done.8
  68.5 0.3 fusion.21
  68.8 0.1 copy.31
  69.0 0.1 convert_element_type.56
  69.1 0.0 copy-start.3
  69.1 0.0 copy-start.5
  69.1 0.0 copy-start.6
  69.1 5.5 %convolution_convert_fusion.1.part = bf16[80,4608]{1,0:T(8,128)(2,1)S(1)} fusion(bf16[80,1024]{1,0:T(8,128)(2,1)S(1)} %convert_element_type.56, bf16[1024,4608]{1,0:T(8,128)(2,1)} %param.22), kind=kOutput, calls=%fused_computation.5 | convolution fusion | flops 755343360 | bytes 10338304 | tf_op jit(solution)/shard_map/dot_general | solution.py:569
  74.6 0.0 copy-done.3
  74.6 0.0 copy-done.5
  74.6 0.0 copy-done.6
  74.6 33.6 %shard_map.168 = (bf16[320,4608]{1,0:T(8,128)(2,1)S(1)}, bf16[80,1152]{1,0:T(8,128)(2,1)S(1)}, f32[4,8,128]{2,1,0:T(8,128)S(1)}) custom-call(bf16[80,4608]{1,0:T(8,128)(2,1)S(1)} %convolution_convert_fusion.1.part, bf16[80,1152]{1,0:T(8,128)(2,1)S(1)} %copy-done.3, f32[1152]{0:T(1024)S(1)} %copy-done.5, f32[1152]{0:T(1024)S(1)} %copy-done.6), custom_call_target="tpu_custom_call" | custom-call | flops 10000000000 | bytes 100000000 | tf_op jit(solution)/shard_map/pallas_call | solution.py:475
  108.3 0.1 mul.169
  108.4 8.3 %fusion.14 = f32[320,1152]{1,0:T(8,128)S(1)} fusion(bf16[320,4608]{1,0:T(8,128)(2,1)S(1)} %get-tuple-element.10, bf16[1152,4608]{1,0:T(8,128)(2,1)} %param.23, f32[320]{0:T(512)S(1)} %mul.169), kind=kOutput, calls=%fused_computation.23 | convolution fusion | flops 3400704000 | bytes 15041792 | tf_op jit(solution)/shard_map/dot_general | solution.py:600
  116.7 0.0 slice-start.2
  116.7 7.2 %fusion.5 = bf16[320,1152]{1,0:T(8,128)(2,1)S(1)} fusion(f32[320,1152]{1,0:T(8,128)S(1)} %fusion.14, bf16[320,4608]{1,0:T(8,128)(2,1)S(1)} %get-tuple-element.10, bf16[1152,4608]{1,0:T(8,128)(2,1)} %param.24, f32[320]{0:T(512)S(1)} %mul.169), kind=kOutput, calls=%fused_computation.9 | convolution fusion | flops 3398492160 | bytes 15779072 | tf_op jit(solution)/shard_map/dot_general | solution.py:601
  123.8 0.0 slice-done
  123.8 0.0 slice-done.1
  123.9 0.0 slice-done.2
  123.9 0.0 copy-start.7
  123.9 4.2 %convolution_convert_fusion.part = bf16[320,4608]{1,0:T(8,128)(2,1)S(1)} fusion(bf16[320,1152]{1,0:T(8,128)(2,1)S(1)} %fusion.5, bf16[1152,4608]{1,0:T(8,128)(2,1)S(1)} %bitcast.67), kind=kOutput, calls=%fused_computation.4 | convolution fusion | flops 3398860800 | bytes 14303232 | tf_op jit(solution)/shard_map/dot_general | solution.py:605
  128.1 0.0 copy-done.7
  128.2 0.0 copy-start.1
  128.2 27.7 %shard_map.169 = bf16[80,1152]{1,0:T(8,128)(2,1)S(1)} custom-call(bf16[320,4608]{1,0:T(8,128)(2,1)S(1)} %convolution_convert_fusion.part, bf16[80,1152]{1,0:T(8,128)(2,1)S(1)} %get-tuple-element.12.mid_ref, f32[1152]{0:T(1024)S(1)} %copy-done.7), custom_call_target="tpu_custom_call" | custom-call | flops 10000000000 | bytes 100000000 | tf_op jit(solution)/shard_map/pallas_call | solution.py:475
  155.9 0.7 copy.56
  156.6 0.0 copy-done.1
  (15 shorter events, 0.2 us)
Async XLA Ops:
  0.6 25.3 %copy-start = (bf16[1152,1024]{1,0:T(8,128)(2,1)S(1)}, bf16[1152,1024]{1,0:T(8,128)(2,1)}, u32[]{:S(2)}) copy-start(bf16[1152,1024]{1,0:T(8,128)(2,1)} %param.19) | copy-start | bytes 7077892
  2.6 0.9 copy-start.2
  3.5 0.7 copy-start.4
  4.2 19.8 %copy-start.9 = (bf16[1152,512]{1,0:T(8,128)(2,1)S(1)}, bf16[1152,512]{1,0:T(8,128)(2,1)}, u32[]{:S(2)}) copy-start(bf16[1152,512]{1,0:T(8,128)(2,1)} %param.21) | copy-start | bytes 3538948
  24.1 1.3 copy-start.10
  56.1 12.3 %copy-start.8 = (bf16[16,5,4,128]{3,2,1,0:T(4,128)(2,1)}, bf16[16,5,4,128]{3,2,1,0:T(4,128)(2,1)S(1)}, u32[]{:S(2)}) copy-start(bf16[16,5,4,128]{3,2,1,0:T(4,128)(2,1)S(1)} %reshape.143) | copy-start | bytes 245764
  57.7 8.8 %slice-start.3 = ((s8[8388608]{0:T(1024)(128)(4,1)}), s8[4194304]{0:T(1024)(128)(4,1)S(1)}, s32[]{:S(2)}) async-start(s8[8388608]{0:T(1024)(128)(4,1)} %bitcast.68), calls=%async_computation.3 | async-start | bytes 8388608
  59.1 7.4 %slice-start.4 = ((s8[8388608]{0:T(1024)(128)(4,1)}), s8[4194304]{0:T(1024)(128)(4,1)S(1)}, s32[]{:S(2)}) async-start(s8[8388608]{0:T(1024)(128)(4,1)} %bitcast.68), calls=%async_computation.4 | async-start | bytes 8388608
  69.1 5.5 %copy-start.3 = (bf16[80,1152]{1,0:T(8,128)(2,1)S(1)}, bf16[80,1152]{1,0:T(8,128)(2,1)}, u32[]{:S(2)}) copy-start(bf16[80,1152]{1,0:T(8,128)(2,1)} %x_ref.3) | copy-start | bytes 552964
  69.1 5.5 %copy-start.5 = (f32[1152]{0:T(1024)S(1)}, f32[1152]{0:T(1024)}, u32[]{:S(2)}) copy-start(f32[1152]{0:T(1024)} %post_ref.2) | copy-start | bytes 13828
  69.1 5.5 %copy-start.6 = (f32[1152]{0:T(1024)S(1)}, f32[1152]{0:T(1024)}, u32[]{:S(2)}) copy-start(f32[1152]{0:T(1024)} %gain_ref.3) | copy-start | bytes 13828
  108.4 15.5 %slice-start = ((s8[10616832]{0:T(1024)(128)(4,1)}), s8[4194304]{0:T(1024)(128)(4,1)S(1)}, s32[]{:S(2)}) async-start(s8[10616832]{0:T(1024)(128)(4,1)} %bitcast.66), calls=%async_computation | async-start | bytes 8388608
  108.4 15.5 %slice-start.1 = ((s8[10616832]{0:T(1024)(128)(4,1)}), s8[4194304]{0:T(1024)(128)(4,1)S(1)}, s32[]{:S(2)}) async-start(s8[10616832]{0:T(1024)(128)(4,1)} %bitcast.66), calls=%async_computation.1 | async-start | bytes 8388608
  116.7 7.2 %slice-start.2 = ((s8[10616832]{0:T(1024)(128)(4,1)}), s8[2228224]{0:T(1024)(128)(4,1)S(1)}, s32[]{:S(2)}) async-start(s8[10616832]{0:T(1024)(128)(4,1)} %bitcast.66), calls=%async_computation.2 | async-start | bytes 4456448
  123.9 4.3 %copy-start.7 = (f32[1152]{0:T(1024)S(1)}, f32[1152]{0:T(1024)}, u32[]{:S(2)}) copy-start(f32[1152]{0:T(1024)} %post_ref.3) | copy-start | bytes 13828
  128.2 28.4 %copy-start.1 = (bf16[1152,1024]{1,0:T(8,128)(2,1)S(1)}, bf16[1152,1024]{1,0:T(8,128)(2,1)}, u32[]{:S(2)}) copy-start(bf16[1152,1024]{1,0:T(8,128)(2,1)} %param.19) | copy-start | bytes 7077892
